TPU v7x, 32 devices: a whole 2x2x4 slice. The times are simulated.
32 devices in a mesh: dp: 8 (over z, core), expert: 4 (over y, x).
Axes of the slice: x: 2, y: 2, z: 4, core: 2. Of those that a mesh axis runs over, the one named last changes fastest.
Arguments:
- patches: bfloat16 [8, 2048, 384], P('dp', 'expert'), may hold values from -6 to 6
- out_grad: bfloat16 [8, 2048, 384], P('dp', 'expert'), may hold values from -6 to 6
- image_of: int32 [8, 2048], P('dp'), may hold values from 0 to 2, never falling along the last dimension, each value on 1 to 1024 neighbouring positions
- task_of: int32 [8, 2048], P('dp', 'expert'), may hold values from 0 to 1
- routes: int32 [8, 2048, 4], P('dp', 'expert'), may hold values from 0 to 15, all different within a row; in each aligned block of 512 rows (0 to 511, 512 to 1023, ..., all dimensions but the last counted through in order) at most 256 rows name the same one
- norm_weight: float32 [4, 384], P(None, 'dp'), may hold values from -0.3 to 1.3, as said below
- norm_moment: float32 [4, 384], P(None, 'dp'), may hold values from -256 to 256
- norm_second: float32 [4, 384], P(None, 'dp'), may hold values from 147.456 to 589.824
- attend_weight: float32 [384, 1152], P('dp'), may hold values from -0.4375 to 0.4375
- attend_moment: float32 [384, 1152], P('dp'), may hold values from -128 to 128
- attend_second: float32 [384, 1152], P('dp'), may hold values from 36.864 to 147.456
- output_weight: float32 [384, 384], P('dp'), may hold values from -1.75 to 1.75
- output_moment: float32 [384, 384], P('dp'), may hold values from -24 to 24
- output_second: float32 [384, 384], P('dp'), may hold values from 1.47456 to 5.89824
- router_weight: float32 [2, 16, 384], P(None, None, 'dp'), may hold values from -0.15625 to 0.15625
- router_moment: float32 [2, 16, 384], P(None, None, 'dp'), may hold values from -320 to 320
- router_second: float32 [2, 16, 384], P(None, None, 'dp'), may hold values from 200.704 to 802.816
- expand_weight: float32 [16, 384, 1536], P('expert'), may hold values from -0.3125 to 0.3125
- expand_moment: float32 [16, 384, 1536], P('expert'), may hold values from -12 to 12
- expand_second: float32 [16, 384, 1536], P('expert'), may hold values from 0.36864 to 1.47456
- reduce_weight: float32 [16, 1536, 384], P('expert'), may hold values from -0.625 to 0.625
- reduce_moment: float32 [16, 1536, 384], P('expert'), may hold values from -4 to 4
- reduce_second: float32 [16, 1536, 384], P('expert'), may hold values from 0.1048576 to 0.4194304
Outputs:
- block_out: bfloat16 [8, 2048, 384], P('dp', 'expert')
- input_grad: float32 [8, 2048, 384], P('dp', 'expert')
- norm_weight_new: float32 [4, 384], P(None, 'dp')
- norm_moment_new: float32 [4, 384], P(None, 'dp')
- norm_second_new: float32 [4, 384], P(None, 'dp')
- attend_weight_new: float32 [384, 1152], P('dp')
- attend_moment_new: float32 [384, 1152], P('dp')
- attend_second_new: float32 [384, 1152], P('dp')
- output_weight_new: float32 [384, 384], P('dp')
- output_moment_new: float32 [384, 384], P('dp')
- output_second_new: float32 [384, 384], P('dp')
- router_weight_new: float32 [2, 16, 384], P(None, None, 'dp')
- router_moment_new: float32 [2, 16, 384], P(None, None, 'dp')
- router_second_new: float32 [2, 16, 384], P(None, None, 'dp')
- expand_weight_new: float32 [16, 384, 1536], P('expert')
- expand_moment_new: float32 [16, 384, 1536], P('expert')
- expand_second_new: float32 [16, 384, 1536], P('expert')
- reduce_weight_new: float32 [16, 1536, 384], P('expert')
- reduce_moment_new: float32 [16, 1536, 384], P('expert')
- reduce_second_new: float32 [16, 1536, 384], P('expert')
Inputs may be any that keep to these rules, and one draw needn't show every extreme that they name: `image_of`: in each row, 3 images of consecutive patches numbered in order from 0, each of 1 to 1024 patches; one has exactly 1024. `routes`: A patch names 4 different experts. Within the rows of one device no expert is named by more than 256 rows, a bound that some block reaches. `norm_weight`: rows 0 and 2 are gains, rows 1 and 3 offsets.
All inputs are finite; a program needn't handle non-finite values.
Results may differ from a plain program's by a relative error of at most 0.024.
Values may be sent and summed in bfloat16 or wider, within the bound.
No kernel may reach another device: no remote copies, remote signals or barrier semaphores. Data moves between devices by JAX's collectives and lax.ppermute only.
A program may use at most 320 MiB of HBM per device.

v0:
```python
import jax
import jax.numpy as jnp
from jax import lax
from jax.sharding import PartitionSpec as P

D = 384
HEADS = 6
HEAD_DIM = 64
EXPERTS = 16
TASKS = 2
TOP = 4
STEP = 10
CAP = 256


NORM_EPS = 1e-06
ADAM_EPS = 1e-08
BETA_FIRST = 0.9
BETA_SECOND = 0.999
DECAY = 0.05
RATE_NORM = 0.5
RATE_ATTEND = 0.2
RATE_OUTPUT = 0.7
RATE_ROUTER = 0.06
RATE_EXPAND = 0.13
RATE_REDUCE = 0.25
MASKED = -1e30


def gelu_exact(values):
    return 0.5 * values * (1.0 + lax.erf(values * 0.7071067811865476))


def norm_rows(values, gain_row, offset):
    average = jnp.mean(values, axis=-1, keepdims=True)
    centred = values - average
    spread = jnp.mean(centred * centred, axis=-1, keepdims=True)
    return centred * lax.rsqrt(spread + NORM_EPS) * gain_row + offset


def adamw(weight, moment, second, gradient, step_rate):
    moment = BETA_FIRST * moment + (1.0 - BETA_FIRST) * gradient
    second = BETA_SECOND * second + (1.0 - BETA_SECOND) * gradient * gradient
    first_hat = moment / (1.0 - BETA_FIRST**STEP)
    second_hat = second / (1.0 - BETA_SECOND**STEP)
    weight = weight - step_rate * (first_hat / (jnp.sqrt(second_hat) + ADAM_EPS) + DECAY * weight)
    return (weight, moment, second)


def body(
    patches,
    out_grad,
    image_of,
    task_of,
    routes,
    norm_weight,
    norm_moment,
    norm_second,
    attend_weight,
    attend_moment,
    attend_second,
    output_weight,
    output_moment,
    output_second,
    router_weight,
    router_moment,
    router_second,
    expand_weight,
    expand_moment,
    expand_second,
    reduce_weight,
    reduce_moment,
    reduce_second,
):
    precise = lax.Precision.HIGHEST
    member = lax.axis_index("expert")
    tokens = patches.shape[1]
    group_rows = image_of.shape[1]
    key_rows = min(512, group_rows)
    score_scale = HEAD_DIM ** (-0.5)
    norm_full, attend_full, output_full, router_full = (
        lax.all_gather(norm_weight.astype(jnp.bfloat16), "dp", axis=1, tiled=True),
        lax.all_gather(attend_weight.astype(jnp.bfloat16), "dp", axis=0, tiled=True),
        lax.all_gather(output_weight.astype(jnp.bfloat16), "dp", axis=0, tiled=True),
        lax.all_gather(router_weight.astype(jnp.bfloat16), "dp", axis=2, tiled=True),
    )
    norm_values = norm_full.astype(jnp.float32)
    router_values = router_full.astype(jnp.float32)
    expand_low = expand_weight.astype(jnp.bfloat16)
    reduce_low = reduce_weight.astype(jnp.bfloat16)
    inputs = patches[0].astype(jnp.float32)
    image_row = image_of[0]
    my_image = lax.dynamic_slice_in_dim(image_row, member * tokens, tokens)
    task_row = task_of[0]
    route_rows = routes[0]
    first_image = my_image[0]
    last_image = my_image[tokens - 1]
    first_key = jnp.sum((image_row < first_image).astype(jnp.int32))
    last_key = jnp.sum((image_row <= last_image).astype(jnp.int32)) - 1
    first_block = first_key // key_rows
    end_block = last_key // key_rows + 1
    normed_one, first_back = jax.vjp(norm_rows, inputs, norm_values[0], norm_values[1])
    normed_low = normed_one.astype(jnp.bfloat16)
    packed = jnp.dot(normed_low, attend_full, preferred_element_type=jnp.float32).astype(
        jnp.bfloat16
    )
    queries = packed[:, :D].reshape(tokens, HEADS, HEAD_DIM)
    key_value = packed[:, D:]
    key_value_all = lax.all_gather(key_value, "expert", axis=0, tiled=True)
    keys_all = key_value_all[:, :D].reshape(group_rows, HEADS, HEAD_DIM)
    values_all = key_value_all[:, D:].reshape(group_rows, HEADS, HEAD_DIM)

    def scores_of(query_part, key_part, same_image):
        raw = (
            jnp.einsum("thd,khd->htk", query_part, key_part, preferred_element_type=jnp.float32)
            * score_scale
        )
        return jnp.where(same_image[None], raw, MASKED)

    def block_at(block_index):
        first_row = block_index * key_rows
        key_part = lax.dynamic_slice_in_dim(keys_all, first_row, key_rows, 0)
        value_part = lax.dynamic_slice_in_dim(values_all, first_row, key_rows, 0)
        same_image = (
            my_image[:, None]
            == lax.dynamic_slice_in_dim(image_row, first_row, key_rows, 0)[None, :]
        )
        return (key_part, value_part, same_image)

    def max_step(block_index, state_in):
        highest, totals = state_in
        key_part, value_part, same_image = block_at(block_index)
        scores = scores_of(queries, key_part, same_image)
        raised = jnp.maximum(highest, jnp.max(scores, axis=-1))
        shares = jnp.where(same_image[None], jnp.exp(scores - raised[..., None]), 0.0)
        return (raised, totals * jnp.exp(highest - raised) + jnp.sum(shares, axis=-1))

    start_max = jnp.full((HEADS, tokens), MASKED, jnp.float32)
    highest, totals = lax.fori_loop(
        first_block, end_block, max_step, (start_max, jnp.zeros((HEADS, tokens), jnp.float32))
    )
    log_total = highest + jnp.log(totals)

    def value_step(block_index, accum):
        key_part, value_part, same_image = block_at(block_index)
        scores = scores_of(queries, key_part, same_image)
        soft_part = jnp.where(same_image[None], jnp.exp(scores - log_total[..., None]), 0.0).astype(
            jnp.bfloat16
        )
        return accum + jnp.einsum(
            "htk,khd->thd", soft_part, value_part, preferred_element_type=jnp.float32
        )

    attended = lax.fori_loop(
        first_block, end_block, value_step, jnp.zeros((tokens, HEADS, HEAD_DIM), jnp.float32)
    )
    attended_low = attended.reshape(tokens, D).astype(jnp.bfloat16)
    branch = jnp.dot(attended_low, output_full, preferred_element_type=jnp.float32)
    middle = inputs + branch
    normed_two, second_back = jax.vjp(norm_rows, middle, norm_values[2], norm_values[3])
    mixed_low = normed_two.astype(jnp.bfloat16)
    task_hot = (task_row[:, None] == jnp.arange(TASKS, dtype=jnp.int32)[None, :]).astype(
        jnp.float32
    )
    route_hot = (
        route_rows[:, :, None] == jnp.arange(EXPERTS, dtype=jnp.int32)[None, None, :]
    ).astype(jnp.float32)

    def gating(hidden, router):
        logits = jnp.einsum("td,ced->tce", hidden, router, precision=precise)
        task_logits = jnp.einsum("tc,tce->te", task_hot, logits, precision=precise)
        chosen = jnp.einsum("te,tke->tk", task_logits, route_hot, precision=precise)
        peak = jnp.max(chosen, axis=-1, keepdims=True)
        raised = jnp.exp(chosen - peak)
        return raised / jnp.sum(raised, axis=-1, keepdims=True)

    gate_values, gate_back = jax.vjp(gating, mixed_low.astype(jnp.float32), router_values)
    pair_expert = route_rows.reshape(-1)
    pair_hot = (pair_expert[:, None] == jnp.arange(EXPERTS, dtype=jnp.int32)[None, :]).astype(
        jnp.int32
    )
    slot_index = jnp.sum((jnp.cumsum(pair_hot, axis=0) - pair_hot) * pair_hot, axis=1)
    flat_slot = pair_expert * CAP + slot_index

    def scatter_pairs(pair_values):
        return (
            jnp.zeros((EXPERTS * CAP, D), pair_values.dtype)
            .at[flat_slot]
            .set(pair_values)
            .reshape(EXPERTS, CAP, D)
        )

    def gather_pairs(buffer):
        return (
            buffer.reshape(EXPERTS * CAP, D)[flat_slot].astype(jnp.float32).reshape(tokens, TOP, D)
        )

    received = lax.all_to_all(
        scatter_pairs(jnp.repeat(mixed_low, TOP, axis=0)),
        "expert",
        split_axis=0,
        concat_axis=1,
        tiled=True,
    )
    hidden_pre = jnp.einsum(
        "ecd,edh->ech", received, expand_low, preferred_element_type=jnp.float32
    )
    active, gelu_back = jax.vjp(gelu_exact, hidden_pre)
    active_low = active.astype(jnp.bfloat16)
    expert_out = jnp.einsum(
        "ech,ehd->ecd", active_low, reduce_low, preferred_element_type=jnp.float32
    ).astype(jnp.bfloat16)
    returned = lax.all_to_all(expert_out, "expert", split_axis=1, concat_axis=0, tiled=True)
    pair_out = gather_pairs(returned)
    expert_mix = jnp.einsum("tk,tkd->td", gate_values, pair_out, precision=precise)
    block_out = (middle + expert_mix).astype(jnp.bfloat16)[None]
    upstream = out_grad[0].astype(jnp.float32)
    gate_grad = jnp.sum(upstream[:, None, :] * pair_out, axis=-1)
    pair_grad = (
        (gate_values[:, :, None] * upstream[:, None, :])
        .astype(jnp.bfloat16)
        .reshape(tokens * TOP, D)
    )
    grad_in = lax.all_to_all(
        scatter_pairs(pair_grad), "expert", split_axis=0, concat_axis=1, tiled=True
    )
    reduce_grad = jnp.einsum(
        "ech,ecd->ehd", active_low, grad_in, preferred_element_type=jnp.float32
    )
    active_grad = jnp.einsum(
        "ecd,ehd->ech", grad_in, reduce_low, preferred_element_type=jnp.float32
    )
    pre_grad = gelu_back(active_grad)[0].astype(jnp.bfloat16)
    expand_grad = jnp.einsum("ecd,ech->edh", received, pre_grad, preferred_element_type=jnp.float32)
    back_rows = jnp.einsum(
        "ech,edh->ecd", pre_grad, expand_low, preferred_element_type=jnp.float32
    ).astype(jnp.bfloat16)
    expand_sum, reduce_sum = (
        lax.psum(expand_grad.astype(jnp.bfloat16), "dp").astype(jnp.float32),
        lax.psum(reduce_grad.astype(jnp.bfloat16), "dp").astype(jnp.float32),
    )
    came_back = lax.all_to_all(back_rows, "expert", split_axis=1, concat_axis=0, tiled=True)
    routed_grad = jnp.sum(gather_pairs(came_back), axis=1)
    hidden_gate_grad, router_grad = gate_back(gate_grad)
    middle_part, gain_two, offset_two = second_back(routed_grad + hidden_gate_grad)
    middle_grad = middle_part + upstream
    branch_grad = middle_grad.astype(jnp.bfloat16)
    output_grad = jnp.einsum(
        "td,te->de", attended_low, branch_grad, preferred_element_type=jnp.float32
    )
    attended_grad = (
        jnp.einsum("te,de->td", branch_grad, output_full, preferred_element_type=jnp.float32)
        .astype(jnp.bfloat16)
        .reshape(tokens, HEADS, HEAD_DIM)
    )
    row_dots = jnp.einsum(
        "thd,thd->ht", attended_grad.astype(jnp.float32), attended, precision=precise
    )

    def score_grad(query_part, key_part, value_part, grad_part, same_image, log_part, dots_part):
        scores = scores_of(query_part, key_part, same_image)
        soft_part = jnp.where(same_image[None], jnp.exp(scores - log_part[..., None]), 0.0)
        soft_grad = jnp.einsum(
            "thd,khd->htk", grad_part, value_part, preferred_element_type=jnp.float32
        )
        return (soft_part, (soft_part * (soft_grad - dots_part[..., None])).astype(jnp.bfloat16))

    def pair_step(block_index, state_in):
        query_acc, terms_acc = state_in
        key_part, value_part, same_image = block_at(block_index)
        soft_part, dscore = score_grad(
            queries, key_part, value_part, attended_grad, same_image, log_total, row_dots
        )
        query_acc = query_acc + jnp.einsum(
            "htk,khd->thd", dscore, key_part, preferred_element_type=jnp.float32
        )
        key_term = (
            jnp.einsum("htk,thd->khd", dscore, queries, preferred_element_type=jnp.float32)
            * score_scale
        )
        value_term = jnp.einsum(
            "htk,thd->khd",
            soft_part.astype(jnp.bfloat16),
            attended_grad,
            preferred_element_type=jnp.float32,
        )
        terms = jnp.concatenate(
            [key_term.reshape(key_rows, D), value_term.reshape(key_rows, D)], axis=1
        )
        terms_acc = lax.dynamic_update_slice_in_dim(terms_acc, terms, block_index * key_rows, 0)
        return (query_acc, terms_acc)

    query_acc, key_value_terms = lax.fori_loop(
        first_block,
        end_block,
        pair_step,
        (
            jnp.zeros((tokens, HEADS, HEAD_DIM), jnp.float32),
            jnp.zeros((group_rows, 2 * D), jnp.float32),
        ),
    )
    key_value_grad = lax.psum_scatter(
        key_value_terms.astype(jnp.bfloat16), "expert", scatter_dimension=0, tiled=True
    ).astype(jnp.float32)
    query_grad = (query_acc * score_scale).reshape(tokens, D)
    packed_grad = jnp.concatenate([query_grad, key_value_grad], axis=1).astype(jnp.bfloat16)
    attend_grad = jnp.einsum(
        "td,te->de", normed_low, packed_grad, preferred_element_type=jnp.float32
    )
    normed_grad = jnp.einsum(
        "te,de->td", packed_grad, attend_full, preferred_element_type=jnp.float32
    )
    input_part, gain_one, offset_one = first_back(normed_grad)
    input_grad = (middle_grad + input_part)[None]
    norm_grad = jnp.stack([gain_one, offset_one, gain_two, offset_two])
    shared = (norm_grad, attend_grad, output_grad, router_grad)
    summed = (
        lax.psum(shared[0].astype(jnp.bfloat16), "expert").astype(jnp.float32),
        lax.psum(shared[1].astype(jnp.bfloat16), "expert").astype(jnp.float32),
        lax.psum(shared[2].astype(jnp.bfloat16), "expert").astype(jnp.float32),
        lax.psum(shared[3].astype(jnp.bfloat16), "expert").astype(jnp.float32),
    )
    norm_sum, attend_sum, output_sum, router_sum = (
        lax.psum_scatter(
            summed[0].astype(jnp.bfloat16), "dp", scatter_dimension=1, tiled=True
        ).astype(jnp.float32),
        lax.psum_scatter(
            summed[1].astype(jnp.bfloat16), "dp", scatter_dimension=0, tiled=True
        ).astype(jnp.float32),
        lax.psum_scatter(
            summed[2].astype(jnp.bfloat16), "dp", scatter_dimension=0, tiled=True
        ).astype(jnp.float32),
        lax.psum_scatter(
            summed[3].astype(jnp.bfloat16), "dp", scatter_dimension=2, tiled=True
        ).astype(jnp.float32),
    )
    norm_new = adamw(norm_weight, norm_moment, norm_second, norm_sum, RATE_NORM)
    attend_new = adamw(attend_weight, attend_moment, attend_second, attend_sum, RATE_ATTEND)
    output_new = adamw(output_weight, output_moment, output_second, output_sum, RATE_OUTPUT)
    router_new = adamw(router_weight, router_moment, router_second, router_sum, RATE_ROUTER)
    expand_new = adamw(expand_weight, expand_moment, expand_second, expand_sum, RATE_EXPAND)
    reduce_new = adamw(reduce_weight, reduce_moment, reduce_second, reduce_sum, RATE_REDUCE)
    return (
        block_out,
        input_grad,
        norm_new[0],
        norm_new[1],
        norm_new[2],
        attend_new[0],
        attend_new[1],
        attend_new[2],
        output_new[0],
        output_new[1],
        output_new[2],
        router_new[0],
        router_new[1],
        router_new[2],
        expand_new[0],
        expand_new[1],
        expand_new[2],
        reduce_new[0],
        reduce_new[1],
        reduce_new[2],
    )


def solution(mesh):
    placed = (
        P("dp", "expert", None),
        P("dp", "expert", None),
        P("dp", None),
        P("dp", "expert"),
        P("dp", "expert", None),
        P(None, "dp"),
        P(None, "dp"),
        P(None, "dp"),
        P("dp", None),
        P("dp", None),
        P("dp", None),
        P("dp", None),
        P("dp", None),
        P("dp", None),
        P(None, None, "dp"),
        P(None, None, "dp"),
        P(None, None, "dp"),
        P("expert", None, None),
        P("expert", None, None),
        P("expert", None, None),
        P("expert", None, None),
        P("expert", None, None),
        P("expert", None, None),
    )
    return jax.shard_map(
        body,
        mesh=mesh,
        in_specs=placed,
        out_specs=(
            P("dp", "expert", None),
            P("dp", "expert", None),
            P(None, "dp"),
            P(None, "dp"),
            P(None, "dp"),
            P("dp", None),
            P("dp", None),
            P("dp", None),
            P("dp", None),
            P("dp", None),
            P("dp", None),
            P(None, None, "dp"),
            P(None, None, "dp"),
            P(None, None, "dp"),
            P("expert", None, None),
            P("expert", None, None),
            P("expert", None, None),
            P("expert", None, None),
            P("expert", None, None),
            P("expert", None, None),
        ),
        check_vma=False,
    )
```

profile of v0, /device:TPU:0, one launch (start us, length us, event | category | flops | bytes accessed | tf_op | source)
XLA Modules:
  0.0 885.1 jit_solution(3553573193019940211)
XLA Ops:
  8.2 17.5 %all_gather.16 = bf16[384,1152]{1,0:T(8,128)(2,1)S(1)} all-gather(bf16[48,1152]{1,0:T(8,128)(2,1)S(1)} %convert_element_type.176), channel_id=1, replica_groups=mesh['dp'=8,'expert'=4] {'dp'}, dimensions={0}, use_global_device_ids=true | all-gather | bytes 995328 | tf_op jit(solution)/shard_map/all_gather | solution.py:83
  27.9 12.0 %all-gather = bf16[8,48,4]{1,2,0:T(4,128)(2,1)S(1)} all-gather(bf16[1,48,4]{1,2,0:T(4,128)(2,1)S(1)} %convert_bitcast_fusion.1), channel_id=1, replica_groups=mesh['dp'=8,'expert'=4] {'dp'}, dimensions={0}, use_global_device_ids=true | all-gather | bytes 3456 | tf_op jit(solution)/shard_map/all_gather | solution.py:82
  42.9 1.9 convert_reduce_fusion.2
  49.3 4.5 reduce-window.6
  54.6 15.4 %all_gather.18 = bf16[384,384]{1,0:T(8,128)(2,1)} all-gather(bf16[48,384]{1,0:T(8,128)(2,1)S(1)} %convert_element_type.180), channel_id=1, replica_groups=mesh['dp'=8,'expert'=4] {'dp'}, dimensions={0}, use_global_device_ids=true | all-gather | bytes 331776 | tf_op jit(solution)/shard_map/all_gather | solution.py:84
  70.6 13.9 %all-gather.3.cloned.1.call-done = bf16[2048,768]{1,0:T(8,128)(2,1)} async-done(((bf16[512,768]{1,0:T(8,128)(2,1)}), bf16[2048,768]{1,0:T(8,128)(2,1)}) %all-gather.3.cloned.1.call-update) | async-done | bytes 3145744 | tf_op jit(solution)/shard_map/all_gather | solution.py:109
  84.5 3.3 fusion.134
  91.2 6.2 while.34
  97.5 7.7 while.35
  97.9 3.4 fusion.195
  101.6 3.4 fusion.195
  109.9 3.7 reshape.371
  113.6 11.9 %scatter_custom_fusion = bf16[4096,384]{1,0:T(8,128)(2,1)} fusion(s32[2048]{0:T(1024)} %bitcast.299, bf16[2048,384]{1,0:T(8,128)(2,1)} %reshape.371, bf16[]{:T(256)} %constant.67.clone.1), kind=kCustom, calls=%fused_computation.84 | custom fusion | bytes 3146240 | tf_op jit(solution)/shard_map/scatter | solution.py:189
  125.5 30.4 %all_to_all.66 = bf16[16,256,384]{2,1,0:T(8,128)(2,1)S(1)} all-to-all(bf16[16,256,384]{2,1,0:T(8,128)(2,1)} %bitcast.268), channel_id=1, replica_groups=mesh['dp'=8,'expert'=4] {'expert'}, dimensions={0} | all-to-all | bytes 6291456 | tf_op jit(solution)/shard_map/all_to_all | solution.py:198
  156.3 16.3 %multiply_convert_fusion = (bf16[4,1024,1536]{2,1,0:T(8,128)(2,1)S(1)}, f32[4,1024,1536]{2,1,0:T(8,128)}) fusion(bf16[4,1024,384]{2,1,0:T(8,128)(2,1)S(1)} %bitcast.263, f32[4,384,1536]{2,1,0:T(8,128)} %param.46), kind=kOutput, calls=%fused_computation.54 | convolution fusion | flops 4865654784 | bytes 50331648 | tf_op jit(solution)/shard_map/ecd,edh->ech/dot_general | solution.py:205
  172.6 12.8 %fusion.60 = bf16[4,1024,384]{2,1,0:T(8,128)(2,1)S(1)} fusion(bf16[4,1024,1536]{2,1,0:T(8,128)(2,1)S(1)} %get-tuple-element.408, f32[4,1536,384]{2,1,0:T(8,128)} %param.49), kind=kOutput, calls=%fused_computation.80 | convolution fusion | flops 4835770368 | bytes 25165824 | tf_op jit(solution)/shard_map/ech,ehd->ecd/dot_general | solution.py:210
  185.3 4.1 copy.149
  189.4 3.7 all-to-all-start.1
  195.1 2.0 bitcast_convert_fusion
  197.0 2.3 copy.152
  199.3 3.3 mul.514
  202.7 4.9 mul.515
  210.3 38.8 %all_gather.19 = bf16[2,16,384]{1,0,2:T(2,128)(2,1)} all-gather(bf16[2,16,48]{1,0,2:T(2,128)(2,1)} %copy.140), channel_id=1, replica_groups=mesh['dp'=8,'expert'=4] {'dp'}, dimensions={2}, use_global_device_ids=true | all-gather | bytes 27648 | tf_op jit(solution)/shard_map/all_gather | solution.py:85
  257.6 3.8 fusion.71
  267.1 2.5 copy.150
  269.6 9.8 %gather_fusion = bf16[2048,384]{1,0:T(8,128)(2,1)} fusion(bf16[4096,384]{1,0:T(8,128)(2,1)S(1)} %bitcast.258, s32[2048]{0:T(1024)} %broadcast_clamp_fusion), kind=kCustom, calls=%fused_computation | custom fusion | bytes 3153920 | tf_op jit(solution)/shard_map/gather | solution.py:195
  279.4 4.0 reshape.340
  283.4 2.5 multiply_reduce_fusion
  285.9 2.4 convert_reduce_fusion.1
  288.3 2.6 fusion.133
  292.7 12.4 %scatter_custom_fusion.1 = bf16[4096,384]{1,0:T(8,128)(2,1)} fusion(s32[2048]{0:T(1024)} %bitcast.301, f32[2048,384]{1,0:T(8,128)S(1)} %copy-done.7, f32[2048]{0:T(1024)} %mul.512, bf16[]{:T(256)} %constant.67.clone.1), kind=kCustom, calls=%fused_computation.81 | custom fusion | flops 1572864 | bytes 6300160 | tf_op jit(solution)/shard_map/scatter | solution.py:189
  305.1 41.8 %all_to_all.67 = bf16[16,256,384]{2,1,0:T(8,128)(2,1)S(1)} all-to-all(bf16[16,256,384]{2,1,0:T(8,128)(2,1)} %bitcast.267), channel_id=1, replica_groups=mesh['dp'=8,'expert'=4] {'expert'}, dimensions={0} | all-to-all | bytes 6291456 | tf_op jit(solution)/shard_map/all_to_all | solution.py:224
  349.0 21.4 %add_convert_fusion = bf16[4,1024,1536]{2,1,0:T(8,128)(2,1)} fusion(f32[4,1024,1536]{2,1,0:T(8,128)} %get-tuple-element.409, bf16[4,1024,384]{2,1,0:T(8,128)(2,1)S(1)} %bitcast.278, f32[4,1536,384]{2,1,0:T(8,128)} %param.49), kind=kOutput, calls=%fused_computation.53 | convolution fusion | flops 4915986432 | bytes 50331648 | tf_op jit(solution)/shard_map/ecd,ehd->ech/dot_general | solution.py:230
  370.4 9.7 %fusion.57 = bf16[4,1024,384]{2,1,0:T(8,128)(2,1)S(1)} fusion(bf16[4,1024,1536]{2,1,0:T(8,128)(2,1)} %add_convert_fusion, f32[4,384,1536]{2,1,0:T(8,128)S(1)} %bitcast.261), kind=kOutput, calls=%fused_computation.79 | convolution fusion | flops 4835770368 | bytes 25165824 | tf_op jit(solution)/shard_map/ech,edh->ecd/dot_general | solution.py:235
  380.1 4.1 copy.154
  384.2 3.7 all-to-all-start.3
  389.9 4.2 fusion.70
  395.8 5.8 fusion.137
  401.6 3.0 copy.179
  404.6 2.1 convolution_convert_fusion.6
  410.1 13.2 %all-to-all-done.3 = bf16[4,1024,384]{2,0,1:T(4,128)(2,1)S(1)} async-done(((bf16[4,1024,384]{2,0,1:T(4,128)(2,1)}), bf16[4,1024,384]{2,0,1:T(4,128)(2,1)S(1)}, u32[]{:S(2)}, u32[]{:S(2)}) %all-to-all-start.3) | async-done | bytes 3145760 | tf_op jit(solution)/shard_map/all_to_all | solution.py:242
  425.0 2.5 copy.155
  427.5 9.8 %gather_fusion.1 = bf16[2048,384]{1,0:T(8,128)(2,1)} fusion(bf16[4096,384]{1,0:T(8,128)(2,1)S(1)} %bitcast.257, s32[2048]{0:T(1024)} %broadcast_clamp_fusion), kind=kCustom, calls=%fused_computation.1 | custom fusion | bytes 3153920 | tf_op jit(solution)/shard_map/gather | solution.py:195
  437.3 4.3 reshape.350
  441.6 3.8 reduce_sum.212
  446.6 2.7 multiply_reduce_fusion.1
  450.0 2.2 fusion.132
  455.9 2.1 broadcast_in_dim.126
  458.0 19.4 %while.36 = (s32[]{:T(128)}, f32[512,6,64]{0,2,1:T(8,128)S(1)}, bf16[2048,768]{0,1:T(8,128)(2,1)}, s32[]{:T(128)}, bf16[2048,6,64]{0,2,1:T(8,128)(2,1)S(1)}, /*i...) while((s32[]{:T(128)}, f32[512,6,64]{0,2,1:T(8,128)S(1)}, ...), condition=%wide.region_27.28_spmd, body=%wide.region_26.27_spmd.sunk | while | flops 1027932160 | bytes 37499188 | solution.py:293
  459.6 3.6 fusion.207
  463.8 1.9 fusion.209
  469.2 3.6 fusion.207
  473.4 1.9 fusion.209
  477.5 10.6 %convolution_convert_fusion.1 = bf16[4,384,1536]{2,1,0:T(8,128)(2,1)} fusion(bf16[4,1024,384]{2,1,0:T(8,128)(2,1)} %bitcast.264, bf16[4,1024,1536]{2,1,0:T(8,128)(2,1)} %add_convert_fusion), kind=kOutput, calls=%fused_computation.67 | convolution fusion | flops 4834197504 | bytes 20447232 | tf_op jit(solution)/shard_map/ecd,ech->edh/dot_general | solution.py:234
  488.1 11.2 %convolution_convert_fusion = bf16[4,1536,384]{2,1,0:T(8,128)(2,1)} fusion(bf16[4,1024,1536]{2,1,0:T(8,128)(2,1)} %copy-done.10, bf16[4,1024,384]{2,1,0:T(8,128)(2,1)S(1)} %bitcast.279), kind=kOutput, calls=%fused_computation.66 | convolution fusion | flops 4834197504 | bytes 20447232 | tf_op jit(solution)/shard_map/ech,ecd->ehd/dot_general | solution.py:227
  502.1 35.8 %reduce-scatter.10.cloned.1.call-done = bf16[512,768]{0,1:T(8,128)(2,1)} async-done(((bf16[2048,768]{0,1:T(8,128)(2,1)}), bf16[512,768]{0,1:T(8,128)(2,1)}) %reduce-scatter.10.cloned.1.call-update) | async-done | bytes 786448 | tf_op jit(solution)/shard_map/reduce_scatter | solution.py:302
  537.9 3.0 fusion.136
  546.0 190.2 %all-reduce.7.cloned.1.call-done = (bf16[4,384,1536]{2,1,0:T(8,128)(2,1)}, bf16[4,1536,384]{2,1,0:T(8,128)(2,1)}) async-done(((bf16[4,384,1536]{2,1,0:T(8,128)(2,1)}, bf16[4,1536,384]{2,1,0:T(8,128)(2,1)}), (bf16[4,384,1536]{2,1,0:T(8,128)(2,1)}, bf16[4,1536,384]{2,1,0:T(8,128)(2,1)})) %all-reduce.7.cloned.1.call-update) | async-done | bytes 9437200 | tf_op jit(solution)/shard_map/psum | solution.py:239
  736.1 23.7 %multiply_subtract_fusion.1 = (f32[4,384,1536]{2,1,0:T(8,128)}, f32[4,384,1536]{2,1,0:T(8,128)}, f32[4,384,1536]{2,1,0:T(8,128)}) fusion(f32[4,384,1536]{2,1,0:T(8,128)} %param.46, bf16[4,384,1536]{2,1,0:T(8,128)(2,1)} %get-tuple-element.368, f32[4,384,1536]{2,1,0:T(8,128)} %param.47, f32[4,384,1536]{2,1,0:T(8,128)} %param.48), kind=kLoop, calls=%fused_computation.65 | loop fusion | flops 37748736 | bytes 61341696 | tf_op jit(solution)/shard_map/sub | solution.py:46
  761.8 23.9 %multiply_subtract_fusion = (f32[4,1536,384]{2,1,0:T(8,128)}, f32[4,1536,384]{2,1,0:T(8,128)}, f32[4,1536,384]{2,1,0:T(8,128)}) fusion(f32[4,1536,384]{2,1,0:T(8,128)} %param.49, bf16[4,1536,384]{2,1,0:T(8,128)(2,1)} %get-tuple-element.369, f32[4,1536,384]{2,1,0:T(8,128)} %param.50, f32[4,1536,384]{2,1,0:T(8,128)} %param.51), kind=kLoop, calls=%fused_computation.64 | loop fusion | flops 37748736 | bytes 61341696 | tf_op jit(solution)/shard_map/sub | solution.py:46
  788.0 12.7 %reduce-scatter.14.cloned.1.call-done = bf16[48,384]{1,0:T(8,128)(2,1)} async-done(((bf16[384,384]{1,0:T(8,128)(2,1)}), bf16[48,384]{1,0:T(8,128)(2,1)}) %reduce-scatter.14.cloned.1.call-update) | async-done | bytes 36880 | tf_op jit(solution)/shard_map/reduce_scatter | solution.py:330
  800.7 17.2 %all-reduce.1 = (bf16[4,48]{1,0:T(4,128)(2,1)S(1)}, bf16[48,384]{1,0:T(8,128)(2,1)S(1)}, bf16[2,16,48]{2,1,0:T(8,128)(2,1)S(1)}) all-reduce(bf16[4,48]{1,0:T(4,128)(2,1)S(1)} %copy.199, bf16[48,384]{1,0:T(8,128)(2,1)} %reduce-scatter.14.cloned.1.call-done, ...), channel_id=1, replica_groups=mesh['dp'=8,'expert'=4] {'expert'}, use_global_device_ids=true, to_apply=%region_35.36 | all-reduce | flops 20160 | bytes 80640 | tf_op jit(solution)/shard_map/psum | solution.py:318
  819.2 14.1 %reduce-scatter.12.cloned.1.call-done = bf16[48,1152]{1,0:T(8,128)(2,1)} async-done(((bf16[384,1152]{1,0:T(8,128)(2,1)}), bf16[48,1152]{1,0:T(8,128)(2,1)}) %reduce-scatter.12.cloned.1.call-update) | async-done | bytes 110608 | tf_op jit(solution)/shard_map/reduce_scatter | solution.py:327
  834.0 42.0 %all-reduce.5.cloned.1.call-done = bf16[48,1152]{1,0:T(8,128)(2,1)} async-done(((bf16[48,1152]{1,0:T(8,128)(2,1)}), bf16[48,1152]{1,0:T(8,128)(2,1)}) %all-reduce.5.cloned.1.call-update) | async-done | bytes 110608 | tf_op jit(solution)/shard_map/psum | solution.py:319
  (287 shorter events, 83.9 us)
Async XLA Ops:
  7.2 35.1 %copy-start.34 = (s32[1,2048]{1,0:T(1,128)S(1)}, s32[1,2048]{1,0:T(1,128)}, u32[]{:S(2)}) copy-start(s32[1,2048]{1,0:T(1,128)} %param.31) | copy-start | bytes 24580
  7.2 41.0 %copy-start.35 = (s32[1,512,4]{1,2,0:T(4,128)S(1)}, s32[1,512,4]{1,2,0:T(4,128)}, u32[]{:S(2)}) copy-start(s32[1,512,4]{1,2,0:T(4,128)} %param.33) | copy-start | bytes 24580
  7.2 41.7 %copy-start.30 = (f32[48,384]{1,0:T(8,128)S(1)}, f32[48,384]{1,0:T(8,128)}, u32[]{:S(2)}) copy-start(f32[48,384]{1,0:T(8,128)} %param.40) | copy-start | bytes 221188
  7.2 77.3 %all-gather.3.cloned.1.call-start = ((), (), s32[]{:S(2)}) async-start(), calls=%async_computation.9 | async-start | bytes 3932160 | tf_op jit(solution)/shard_map/all_gather | solution.py:109
  25.7 62.1 %copy-start.26 = (bf16[384,1152]{1,0:T(8,128)(2,1)}, bf16[384,1152]{1,0:T(8,128)(2,1)S(1)}, u32[]{:S(2)}) copy-start(bf16[384,1152]{1,0:T(8,128)(2,1)S(1)} %all_gather.16) | copy-start | bytes 2654212
  27.2 78.2 %copy-start.4 = (bf16[1,512,384]{1,2,0:T(8,128)(2,1)}, bf16[1,512,384]{1,2,0:T(8,128)(2,1)S(1)}, u32[]{:S(2)}) copy-start(bf16[1,512,384]{1,2,0:T(8,128)(2,1)S(1)} %copy.135) | copy-start | bytes 1179652
  40.0 14.4 %copy-start.42 = (f32[384]{0:T(512)}, f32[384]{0:T(512)S(1)}, u32[]{:S(2)}) copy-start(f32[384]{0:T(512)S(1)} %get-tuple-element.309) | copy-start | bytes 4612
  40.1 47.8 %copy-start.60 = (f32[384]{0:T(512)}, f32[384]{0:T(512)S(1)}, u32[]{:S(2)}) copy-start(f32[384]{0:T(512)S(1)} %get-tuple-element.308) | copy-start | bytes 4612
  40.1 67.1 %copy-start.44 = (f32[384]{0:T(512)}, f32[384]{0:T(512)S(1)}, u32[]{:S(2)}) copy-start(f32[384]{0:T(512)S(1)} %get-tuple-element.306) | copy-start | bytes 4612
  40.2 14.3 %copy-start.39 = (f32[512]{0:T(512)}, f32[512]{0:T(512)S(1)}, u32[]{:S(2)}) copy-start(f32[512]{0:T(512)S(1)} %broadcast_multiply_fusion.2) | copy-start | bytes 6148
  40.3 7.8 copy-start.49
  40.3 7.8 copy-start.46
  105.3 1.9 copy-start.53
  105.3 20.2 %copy-start = (bf16[2048,6,64]{0,2,1:T(8,128)(2,1)}, bf16[2048,6,64]{0,2,1:T(8,128)(2,1)S(1)}, u32[]{:S(2)}) copy-start(bf16[2048,6,64]{0,2,1:T(8,128)(2,1)S(1)} %get-tuple-element.734) | copy-start | bytes 4718596
  105.3 20.2 %copy-start.11 = (f32[512,6,64]{0,2,1:T(8,128)}, f32[512,6,64]{0,2,1:T(8,128)S(1)}, u32[]{:S(2)}) copy-start(f32[512,6,64]{0,2,1:T(8,128)S(1)} %get-tuple-element.178) | copy-start | bytes 2359300
  108.1 47.9 %copy-start.16 = (bf16[512,384]{0,1:T(8,128)(2,1)}, bf16[512,384]{0,1:T(8,128)(2,1)S(1)}, u32[]{:S(2)}) copy-start(bf16[512,384]{0,1:T(8,128)(2,1)S(1)} %add_convert_fusion.1) | copy-start | bytes 1179652
  156.3 16.3 %copy-start.6 = (bf16[4,4,256,384]{3,2,1,0:T(8,128)(2,1)}, bf16[4,4,256,384]{3,2,1,0:T(8,128)(2,1)S(1)}, u32[]{:S(2)}) copy-start(bf16[4,4,256,384]{3,2,1,0:T(8,128)(2,1)S(1)} %copy.148) | copy-start | bytes 9437188
  172.6 12.8 %copy-start.10 = (bf16[4,1024,1536]{2,1,0:T(8,128)(2,1)}, bf16[4,1024,1536]{2,1,0:T(8,128)(2,1)S(1)}, u32[]{:S(2)}) copy-start(bf16[4,1024,1536]{2,1,0:T(8,128)(2,1)S(1)} %get-tuple-element.408) | copy-start | bytes 37748740
  189.4 76.0 %all-to-all-start.1 = ((bf16[4,1024,384]{2,0,1:T(4,128)(2,1)}), bf16[4,1024,384]{2,0,1:T(4,128)(2,1)S(1)}, u32[]{:S(2)}, u32[]{:S(2)}) async-start(bf16[4,1024,384]{2,0,1:T(4,128)(2,1)} %copy.149), calls=%async_computation.1 | async-start | bytes 6291456 | tf_op jit(solution)/shard_map/all_to_all | solution.py:213
  279.4 13.3 %copy-start.7 = (f32[2048,384]{1,0:T(8,128)S(1)}, f32[2048,384]{1,0:T(8,128)}, u32[]{:S(2)}) copy-start(f32[2048,384]{1,0:T(8,128)} %mul.515) | copy-start | bytes 9437188
  346.9 23.5 %slice-start = ((s8[9437184]{0:T(1024)(128)(4,1)}), s8[4194304]{0:T(1024)(128)(4,1)S(1)}, s32[]{:S(2)}) async-start(s8[9437184]{0:T(1024)(128)(4,1)} %bitcast.260), calls=%async_computation.17 | async-start | bytes 8388608
  349.0 21.4 %slice-start.1 = ((s8[9437184]{0:T(1024)(128)(4,1)}), s8[4194304]{0:T(1024)(128)(4,1)S(1)}, s32[]{:S(2)}) async-start(s8[9437184]{0:T(1024)(128)(4,1)} %bitcast.260), calls=%async_computation.18 | async-start | bytes 8388608
  349.0 21.4 %slice-start.2 = ((s8[9437184]{0:T(1024)(128)(4,1)}), s8[1048576]{0:T(1024)(128)(4,1)S(1)}, s32[]{:S(2)}) async-start(s8[9437184]{0:T(1024)(128)(4,1)} %bitcast.260), calls=%async_computation.19 | async-start | bytes 2097152
  384.2 39.1 %all-to-all-start.3 = ((bf16[4,1024,384]{2,0,1:T(4,128)(2,1)}), bf16[4,1024,384]{2,0,1:T(4,128)(2,1)S(1)}, u32[]{:S(2)}, u32[]{:S(2)}) async-start(bf16[4,1024,384]{2,0,1:T(4,128)(2,1)} %copy.154), calls=%async_computation.3 | async-start | bytes 6291456 | tf_op jit(solution)/shard_map/all_to_all | solution.py:242
  387.9 111.8 %reduce-scatter.18.cloned.1.call-start = ((), (), s32[]{:S(2)}) async-start(), calls=%async_computation.15 | async-start | bytes 110592
  410.0 127.9 %reduce-scatter.10.cloned.1.call-start = ((), (), s32[]{:S(2)}) async-start(), calls=%async_computation.10 | async-start | bytes 3932160 | tf_op jit(solution)/shard_map/reduce_scatter | solution.py:302
  437.3 9.3 %copy-start.3 = (f32[512,384]{0,1:T(8,128)S(1)}, f32[512,384]{0,1:T(8,128)}, u32[]{:S(2)}) copy-start(f32[512,384]{0,1:T(8,128)} %copy-done.2) | copy-start | bytes 2359300
  441.6 13.5 %copy-start.12 = (f32[512,6,64]{0,2,1:T(8,128)S(1)}, f32[512,6,64]{0,2,1:T(8,128)}, u32[]{:S(2)}) copy-start(f32[512,6,64]{0,2,1:T(8,128)} %copy-done.11) | copy-start | bytes 2359300
  446.6 11.4 %copy-start.1 = (bf16[2048,6,64]{0,2,1:T(8,128)(2,1)S(1)}, bf16[2048,6,64]{0,2,1:T(8,128)(2,1)}, u32[]{:S(2)}) copy-start(bf16[2048,6,64]{0,2,1:T(8,128)(2,1)} %copy-done) | copy-start | bytes 4718596
  452.2 3.7 copy-start.13
  453.6 2.2 copy-start.17
  477.4 258.7 %all-reduce.7.cloned.1.call-start = ((), (), s32[]{:S(2)}) async-start(), calls=%async_computation.16 | async-start | bytes 18874368 | tf_op jit(solution)/shard_map/psum | solution.py:239
  477.5 10.6 %copy-start.22 = (bf16[4,4,256,384]{3,2,1,0:T(8,128)(2,1)S(1)}, bf16[4,4,256,384]{3,2,1,0:T(8,128)(2,1)}, u32[]{:S(2)}) copy-start(bf16[4,4,256,384]{3,2,1,0:T(8,128)(2,1)} %copy-done.21) | copy-start | bytes 9437188
  499.3 2.0 copy-start.58
  499.3 38.6 %copy-start.27 = (bf16[384,1152]{1,0:T(8,128)(2,1)S(1)}, bf16[384,1152]{1,0:T(8,128)(2,1)}, u32[]{:S(2)}) copy-start(bf16[384,1152]{1,0:T(8,128)(2,1)} %copy-done.26) | copy-start | bytes 2654212
  499.3 43.0 %copy-start.5 = (bf16[1,512,384]{1,2,0:T(8,128)(2,1)S(1)}, bf16[1,512,384]{1,2,0:T(8,128)(2,1)}, u32[]{:S(2)}) copy-start(bf16[1,512,384]{1,2,0:T(8,128)(2,1)} %copy-done.4) | copy-start | bytes 1179652
  499.3 43.0 %copy-start.40 = (f32[512]{0:T(512)S(1)}, f32[512]{0:T(512)}, u32[]{:S(2)}) copy-start(f32[512]{0:T(512)} %copy-done.39) | copy-start | bytes 6148
  499.3 43.0 %copy-start.43 = (f32[384]{0:T(512)S(1)}, f32[384]{0:T(512)}, u32[]{:S(2)}) copy-start(f32[384]{0:T(512)} %copy-done.42) | copy-start | bytes 4612
  499.4 43.1 %copy-start.50 = (f32[512]{0:T(512)S(1)}, f32[512]{0:T(512)}, u32[]{:S(2)}) copy-start(f32[512]{0:T(512)} %copy-done.49) | copy-start | bytes 6148
  499.4 43.2 %copy-start.47 = (f32[512]{0:T(512)S(1)}, f32[512]{0:T(512)}, u32[]{:S(2)}) copy-start(f32[512]{0:T(512)} %copy-done.46) | copy-start | bytes 6148
  499.4 44.4 %copy-start.18 = (bf16[512,384]{0,1:T(8,128)(2,1)S(1)}, bf16[512,384]{0,1:T(8,128)(2,1)}, u32[]{:S(2)}) copy-start(bf16[512,384]{0,1:T(8,128)(2,1)} %copy-done.17) | copy-start | bytes 1179652
  499.4 44.4 %copy-start.20 = (bf16[512,6,64]{0,2,1:T(8,128)(2,1)S(1)}, bf16[512,6,64]{0,2,1:T(8,128)(2,1)}, u32[]{:S(2)}) copy-start(bf16[512,6,64]{0,2,1:T(8,128)(2,1)} %copy-done.19) | copy-start | bytes 1179652
  499.4 45.6 %copy-start.23 = (bf16[1,512,384]{1,2,0:T(8,128)(2,1)S(1)}, bf16[1,512,384]{1,2,0:T(8,128)(2,1)}, u32[]{:S(2)}) copy-start(bf16[1,512,384]{1,2,0:T(8,128)(2,1)} %get-tuple-element.401) | copy-start | bytes 1179652
  499.4 287.8 %reduce-scatter.16.cloned.1.call-start = ((), (), s32[]{:S(2)}) async-start(), calls=%async_computation.14 | async-start | bytes 110592
  543.8 256.9 %reduce-scatter.14.cloned.1.call-start = ((), (), s32[]{:S(2)}) async-start(), calls=%async_computation.13 | async-start | bytes 331776 | tf_op jit(solution)/shard_map/reduce_scatter | solution.py:330
  545.9 287.4 %reduce-scatter.12.cloned.1.call-start = ((), (), s32[]{:S(2)}) async-start(), calls=%async_computation.11 | async-start | bytes 995328 | tf_op jit(solution)/shard_map/reduce_scatter | solution.py:327
  736.1 23.8 %copy-start.29 = (bf16[512,6,64]{0,2,1:T(8,128)(2,1)S(1)}, bf16[512,6,64]{0,2,1:T(8,128)(2,1)}, u32[]{:S(2)}) copy-start(bf16[512,6,64]{0,2,1:T(8,128)(2,1)} %multiply_convert_fusion.3) | copy-start | bytes 1179652
  736.1 23.8 %copy-start.61 = (f32[384]{0:T(512)S(1)}, f32[384]{0:T(512)}, u32[]{:S(2)}) copy-start(f32[384]{0:T(512)} %copy-done.60) | copy-start | bytes 4612
  736.1 23.8 %copy-start.64 = (bf16[512,768]{0,1:T(8,128)(2,1)S(1)}, bf16[512,768]{0,1:T(8,128)(2,1)}, u32[]{:S(2)}) copy-start(bf16[512,768]{0,1:T(8,128)(2,1)} %reduce-scatter.10.cloned.1.call-done) | copy-start | bytes 2359300
  761.6 114.4 %all-reduce.5.cloned.1.call-start = ((), (), s32[]{:S(2)}) async-start(), calls=%async_computation.12 | async-start | bytes 221184 | tf_op jit(solution)/shard_map/psum | solution.py:319
  761.6 24.0 %copy-start.14 = (f32[512,384]{0,1:T(8,128)S(1)}, f32[512,384]{0,1:T(8,128)}, u32[]{:S(2)}) copy-start(f32[512,384]{0,1:T(8,128)} %copy-done.13) | copy-start | bytes 2359300
  761.6 24.0 %copy-start.15 = (bf16[1,512,384]{1,2,0:T(8,128)(2,1)S(1)}, bf16[1,512,384]{1,2,0:T(8,128)(2,1)}, u32[]{:S(2)}) copy-start(bf16[1,512,384]{1,2,0:T(8,128)(2,1)} %copy.151) | copy-start | bytes 1179652
  761.6 56.2 %copy-start.38 = (f32[2,16,48]{2,1,0:T(8,128)S(1)}, f32[2,16,48]{2,1,0:T(8,128)}, u32[]{:S(2)}) copy-start(f32[2,16,48]{2,1,0:T(8,128)} %param.43) | copy-start | bytes 18436
  761.7 56.2 %copy-start.55 = (f32[2,16,48]{2,1,0:T(8,128)S(1)}, f32[2,16,48]{2,1,0:T(8,128)}, u32[]{:S(2)}) copy-start(f32[2,16,48]{2,1,0:T(8,128)} %param.44) | copy-start | bytes 18436
  761.7 56.2 %copy-start.56 = (f32[2,16,48]{2,1,0:T(8,128)S(1)}, f32[2,16,48]{2,1,0:T(8,128)}, u32[]{:S(2)}) copy-start(f32[2,16,48]{2,1,0:T(8,128)} %param.45) | copy-start | bytes 18436
  761.7 56.8 %copy-start.31 = (f32[48,384]{1,0:T(8,128)S(1)}, f32[48,384]{1,0:T(8,128)}, u32[]{:S(2)}) copy-start(f32[48,384]{1,0:T(8,128)} %param.40) | copy-start | bytes 221188
  761.7 56.8 %copy-start.36 = (f32[48,384]{1,0:T(8,128)S(1)}, f32[48,384]{1,0:T(8,128)}, u32[]{:S(2)}) copy-start(f32[48,384]{1,0:T(8,128)} %param.41) | copy-start | bytes 221188
  761.7 56.8 %copy-start.37 = (f32[48,384]{1,0:T(8,128)S(1)}, f32[48,384]{1,0:T(8,128)}, u32[]{:S(2)}) copy-start(f32[48,384]{1,0:T(8,128)} %param.42) | copy-start | bytes 221188
  761.7 71.6 %copy-start.57 = (f32[4,48]{1,0:T(4,128)S(1)}, f32[4,48]{1,0:T(4,128)}, u32[]{:S(2)}) copy-start(f32[4,48]{1,0:T(4,128)} %param.34) | copy-start | bytes 2308
  761.7 71.6 %copy-start.62 = (f32[4,48]{1,0:T(4,128)S(1)}, f32[4,48]{1,0:T(4,128)}, u32[]{:S(2)}) copy-start(f32[4,48]{1,0:T(4,128)} %param.35) | copy-start | bytes 2308
  761.7 71.6 %copy-start.63 = (f32[4,48]{1,0:T(4,128)S(1)}, f32[4,48]{1,0:T(4,128)}, u32[]{:S(2)}) copy-start(f32[4,48]{1,0:T(4,128)} %param.36) | copy-start | bytes 2308
  761.8 114.2 %copy-start.28 = (f32[48,1152]{1,0:T(8,128)S(1)}, f32[48,1152]{1,0:T(8,128)}, u32[]{:S(2)}) copy-start(f32[48,1152]{1,0:T(8,128)} %param.37) | copy-start | bytes 663556
  761.8 114.2 %copy-start.32 = (f32[48,1152]{1,0:T(8,128)S(1)}, f32[48,1152]{1,0:T(8,128)}, u32[]{:S(2)}) copy-start(f32[48,1152]{1,0:T(8,128)} %param.38) | copy-start | bytes 663556
  761.8 114.2 %copy-start.33 = (f32[48,1152]{1,0:T(8,128)S(1)}, f32[48,1152]{1,0:T(8,128)}, u32[]{:S(2)}) copy-start(f32[48,1152]{1,0:T(8,128)} %param.39) | copy-start | bytes 663556
  (17 other events, 21.5 us)
Sparse Core Ops, SparseCore 0:
  42.4 42.0 all-gather.2
  410.2 29.2 reduce-scatter.17
  477.5 60.3 reduce-scatter.9
  540.8 195.3 all-reduce.6
  738.8 30.6 reduce-scatter.15
  771.6 29.0 reduce-scatter.13
  803.0 30.3 reduce-scatter.11
  836.2 39.7 all-reduce.4
where the time goes:
time: 889 us; the launch traced here: 885 us
  waiting for transfers between devices  322 us (36%)
  blocking collectives  173 us (19%)
  matrix products  138 us (16%)
  local copies, waits for them, and re-layouts  116 us (13%)
  other arithmetic  108 us (12%)
  between operations  18.9 us (2%)
    psum x1, waiting for transfers between devices, body(): lax.psum(expand_grad.astype(jnp.bfloat16), 'dp').astype(jnp.float32)  190 us
    sub x6, other arithmetic, adamw(): weight - step_rate * (first_hat / (jnp.sqrt(second_hat) + ADAM_EPS) + DEC...  51.4 us
    psum x1, waiting for transfers between devices, body(): lax.psum(shared[1].astype(jnp.bfloat16), 'expert').astype(jnp.float32)  42 us
    all_to_all x1, blocking collectives, body(): lax.all_to_all(scatter_pairs(pair_grad), 'expert', split_axis=0, concat_a...  41.8 us
    all_gather x1, blocking collectives, body(): lax.all_gather(router_weight.astype(jnp.bfloat16), 'dp', axis=2, tiled=True)  38.8 us
    reduce_scatter x1, waiting for transfers between devices, body(): lax.psum_scatter(key_value_terms.astype(jnp.bfloat16), 'expert', scatter_...  35.8 us
    all_to_all x1, blocking collectives, body(): lax.all_to_all(scatter_pairs(jnp.repeat(mixed_low, TOP, axis=0)), 'expert...  30.4 us
    dot_general x1, matrix products, body(): jnp.einsum('ecd,ehd->ech', grad_in, reduce_low, preferred_element_type=jn...  21.4 us
  transfers between devices with their start and end apart: 10, of which 7 were waited for; matrix products, arithmetic and copies ran while one was open for 23% of the time, Pallas kernels for 0%

commit v1 on v0

--- a/solution.py
+++ b/solution.py
@@ -1,17 +1,27 @@
+import functools
+
 import jax
 import jax.numpy as jnp
 from jax import lax
+from jax.experimental import pallas as pl
+from jax.experimental.pallas import tpu as pltpu
 from jax.sharding import PartitionSpec as P
 
 D = 384
 HEADS = 6
 HEAD_DIM = 64
+FFN = 1536
 EXPERTS = 16
 TASKS = 2
 TOP = 4
 STEP = 10
 CAP = 256
-
+PAIRS = HEADS // 2
+LANES = 128
+WCOLS = 4 * D + LANES
+INFO = 16
+NORM_AT = 2 * EXPERTS
+EXTRA = 64
 
 NORM_EPS = 1e-06
 ADAM_EPS = 1e-08
@@ -25,17 +35,583 @@
 RATE_EXPAND = 0.13
 RATE_REDUCE = 0.25
 MASKED = -1e30
-
-
-def gelu_exact(values):
-    return 0.5 * values * (1.0 + lax.erf(values * 0.7071067811865476))
-
-
-def norm_rows(values, gain_row, offset):
+F32 = jnp.float32
+BF16 = jnp.bfloat16
+
+
+def dot_nn(a, b):
+    return lax.dot_general(a, b, (((1,), (0,)), ((), ())), preferred_element_type=F32)
+
+
+def dot_nt(a, b):
+    return lax.dot_general(a, b, (((1,), (1,)), ((), ())), preferred_element_type=F32)
+
+
+def dot_tn(a, b):
+    return lax.dot_general(a, b, (((0,), (0,)), ((), ())), preferred_element_type=F32)
+
+
+def unit_rows(values):
     average = jnp.mean(values, axis=-1, keepdims=True)
     centred = values - average
     spread = jnp.mean(centred * centred, axis=-1, keepdims=True)
-    return centred * lax.rsqrt(spread + NORM_EPS) * gain_row + offset
+    scale = lax.rsqrt(spread + NORM_EPS)
+    return centred * scale, scale
+
+
+def eye(n):
+    rows = lax.broadcasted_iota(jnp.int32, (n, n), 0)
+    cols = lax.broadcasted_iota(jnp.int32, (n, n), 1)
+    return (rows == cols).astype(F32).astype(BF16)
+
+
+def norm_rows_of(full_ref):
+    return dot_nt(eye(LANES), full_ref[:, 4 * D :])[NORM_AT : NORM_AT + 8]
+
+
+def vmem():
+    return pl.BlockSpec(memory_space=pltpu.VMEM)
+
+
+def smem():
+    return pl.BlockSpec(memory_space=pltpu.SMEM)
+
+
+def route_kernel(meta, i0, i1, i2, i3, row_out, col_out, plan_out):
+    base = meta[0]
+    rows = i0.shape[1] + LANES
+    later = lax.broadcasted_iota(jnp.int32, (rows, rows), 0)
+    token = lax.broadcasted_iota(jnp.int32, (rows, rows), 1)
+    before = (later < token).astype(F32).astype(BF16)
+    one = (later == token).astype(F32).astype(BF16)
+    local = row_out.shape[0]
+    which = lax.broadcasted_iota(jnp.int32, (local, rows), 0)
+    slot_names = (which + base).astype(F32)
+    every = lax.broadcasted_iota(jnp.int32, (EXPERTS, rows), 0).astype(F32)
+    experts = plan_out.shape[0] // 8
+    starts = [jnp.int32(0)] * experts
+    for d, ref in enumerate((i0, i1, i2, i3)):
+        info = ref[...].astype(F32)
+
+        def line(k):
+            return jnp.concatenate([info[2 * k : 2 * k + 1], info[2 * k + 1 : 2 * k + 2, :LANES]], axis=1)
+
+        mine = jnp.zeros((local, rows), jnp.bool_)
+        chosen = jnp.zeros((EXPERTS, rows), jnp.bool_)
+        for k in range(TOP):
+            named = line(k)
+            mine = mine | (slot_names == named)
+            chosen = chosen | (every == named)
+        mine = jnp.where(mine & (which < experts), 1.0, 0.0)
+        chosen = jnp.where(chosen, 1.0, 0.0)
+        rank = dot_nn(mine.astype(BF16), before)
+        spot = jnp.where(mine > 0.5, rank, -1.0)
+        row_out[:, d * rows : (d + 1) * rows] = spot
+        tasks = jnp.broadcast_to(line(TOP), (8, rows))
+        table = jnp.concatenate(
+            [spot, jnp.zeros((16 - local, rows), F32), chosen, tasks, jnp.zeros((LANES - 40, rows), F32)],
+            axis=0,
+        )
+        col_out[d * rows : (d + 1) * rows, :] = dot_nt(one, table.astype(BF16))
+        for e in range(experts):
+            held = jnp.sum(mine[e : e + 1, :]).astype(jnp.int32)
+            plan_out[e * 8 + d] = starts[e]
+            starts[e] = starts[e] + (held + 15) // 16 * 16
+    for e in range(experts):
+        plan_out[e * 8 + 4] = starts[e]
+        plan_out[e * 8 + 5] = (starts[e] + CAP - 1) // CAP
+
+
+def route_call(meta, pieces, experts):
+    rows = pieces[0].shape[0] - INFO
+    return pl.pallas_call(
+        route_kernel,
+        grid=(1,),
+        in_specs=[smem()] + [pl.BlockSpec((INFO, D), lambda i: (rows // INFO, 0))] * 4,
+        out_specs=(
+            pl.BlockSpec((8, 4 * rows), lambda i: (0, 0)),
+            pl.BlockSpec((4 * rows, LANES), lambda i: (0, 0)),
+            smem(),
+        ),
+        out_shape=(
+            jax.ShapeDtypeStruct((8, 4 * rows), F32),
+            jax.ShapeDtypeStruct((4 * rows, LANES), F32),
+            jax.ShapeDtypeStruct((experts * 8,), jnp.int32),
+        ),
+        name="routing",
+    )(meta, *pieces)
+
+
+def front_kernel(
+    meta, image, p0, p1, p2, p3, w0, w1, w2, w3, w4, w5, w6, w7,
+    qkv, full, att, lse_col, lse_row, middle, mixed,
+    everything, scores, top, total, out_acc,
+):
+    rows = att.shape[0]
+    for j, ref in enumerate((w0, w1, w2, w3, w4, w5, w6, w7)):
+        full[pl.ds(pl.multiple_of(meta[16 + j], 16), ref.shape[0]), :] = ref[...]
+    for d, ref in enumerate((p0, p1, p2, p3)):
+        everything[d * rows : (d + 1) * rows, :] = ref[:rows, :]
+    norms = norm_rows_of(full)
+    tile = 256
+
+    def project(i, carry):
+        at = pl.ds(pl.multiple_of(i * tile, tile), tile)
+        unit, _ = unit_rows(everything[at, :].astype(F32))
+        normed = (unit * norms[0:1] + norms[1:2]).astype(BF16)
+        for third in range(3):
+            made = dot_nn(normed, full[:, third * D : (third + 1) * D]).astype(BF16)
+            if third == 0:
+                made = made * jnp.asarray(HEAD_DIM ** (-0.5), BF16)
+            for part in range(PAIRS):
+                qkv[third * PAIRS + part, at, :] = made[:, part * LANES : (part + 1) * LANES]
+        return carry
+
+    lax.fori_loop(0, 4 * rows // tile, project, 0)
+    own_row = image[pl.ds(meta[4], 1), :].astype(F32)
+    own_col = jnp.transpose(jnp.broadcast_to(own_row, (LANES, rows)))[:, :1]
+    lane = lax.broadcasted_iota(jnp.int32, (rows, LANES), 1)
+    lse_col[...] = jnp.zeros_like(lse_col)
+
+    def pair_of_heads(pair, carry):
+        done = []
+        for half in range(2):
+            held = (lane < HEAD_DIM) if half == 0 else (lane >= HEAD_DIM)
+            query = jnp.where(held, qkv[pair, 0:rows, :], jnp.zeros((), BF16))
+            top[...] = jnp.full_like(top, MASKED)
+
+            def score(d, c):
+                @pl.when(meta[8 + d] > 0)
+                def _():
+                    key = qkv[PAIRS + pair, pl.ds(pl.multiple_of(d * rows, rows), rows), :]
+                    same = own_col == image[pl.ds(meta[4 + d], 1), :].astype(F32)
+                    raw = jnp.where(same, dot_nt(query, key), MASKED)
+                    scores[d] = raw
+                    top[...] = jnp.maximum(top[...], jnp.max(raw, axis=1, keepdims=True))
+
+                return c
+
+            lax.fori_loop(0, 4, score, 0)
+            total[...] = jnp.zeros_like(total)
+            out_acc[...] = jnp.zeros_like(out_acc)
+            peak = top[:, :1]
+
+            def weigh(d, c):
+                @pl.when(meta[8 + d] > 0)
+                def _():
+                    value = qkv[2 * PAIRS + pair, pl.ds(pl.multiple_of(d * rows, rows), rows), :]
+                    shares = jnp.exp(scores[d] - peak)
+                    total[...] += jnp.sum(shares, axis=1, keepdims=True)
+                    out_acc[...] += dot_nn(shares.astype(BF16), value)
+
+                return c
+
+            lax.fori_loop(0, 4, weigh, 0)
+            done.append(out_acc[...] / total[:, :1])
+            lse_col[...] = jnp.where(lane == 2 * pair + half, peak + jnp.log(total[:, :1]), lse_col[...])
+        att[:, pl.ds(pl.multiple_of(pair * LANES, LANES), LANES)] = jnp.where(lane < HEAD_DIM, done[0], done[1])
+        return carry
+
+    lax.fori_loop(0, PAIRS, pair_of_heads, 0)
+    lse_row[...] = jnp.transpose(lse_col[...])[:8]
+    branch = dot_nn(att[...].astype(BF16), full[:, 3 * D : 4 * D])
+    centre = everything[0:rows, :].astype(F32) + branch
+    middle[...] = centre
+    unit, _ = unit_rows(centre)
+    mixed[...] = (unit * norms[2:3] + norms[3:4]).astype(BF16)
+
+
+def front_call(meta, image, pieces, shards):
+    rows = pieces[0].shape[0] - INFO
+    return pl.pallas_call(
+        front_kernel,
+        in_specs=[smem()] + [vmem()] * 13,
+        out_specs=(vmem(),) * 7,
+        out_shape=(
+            jax.ShapeDtypeStruct((3 * PAIRS, 4 * rows, LANES), BF16),
+            jax.ShapeDtypeStruct((D, WCOLS), BF16),
+            jax.ShapeDtypeStruct((rows, D), F32),
+            jax.ShapeDtypeStruct((rows, LANES), F32),
+            jax.ShapeDtypeStruct((8, rows), F32),
+            jax.ShapeDtypeStruct((rows, D), F32),
+            jax.ShapeDtypeStruct((rows, D), BF16),
+        ),
+        scratch_shapes=[
+            pltpu.VMEM((4 * rows, D), BF16),
+            pltpu.VMEM((4, rows, rows), F32),
+            pltpu.VMEM((rows, 1), F32),
+            pltpu.VMEM((rows, 1), F32),
+            pltpu.VMEM((rows, LANES), F32),
+        ],
+        name="front",
+    )(meta, image, *pieces, *shards)
+
+
+def expert_kernel(
+    plan, meta, m0, m1, m2, m3, g0, g1, g2, g3, spot_row, spot_col, full, up, down,
+    mine, other, back_out, mix_out, router_out,
+    gates, terms, back_acc, mix_acc, hidden, upstream, results, low_up, low_down, sum_up, sum_down,
+):
+    step = pl.program_id(0)
+    last = pl.num_programs(0) - 1
+    base, core = meta[0], meta[1]
+    rows = m0.shape[0]
+    lane = lax.broadcasted_iota(jnp.int32, (rows, LANES), 1)
+
+    @pl.when(step == 0)
+    def _():
+        hidden[...] = jnp.zeros_like(hidden)
+        upstream[...] = jnp.zeros_like(upstream)
+        results[...] = jnp.zeros_like(results)
+        terms[...] = jnp.zeros_like(terms)
+        back_acc[...] = jnp.zeros_like(back_acc)
+        mix_acc[...] = jnp.zeros_like(mix_acc)
+        for d, ref in enumerate((m0, m1, m2, m3)):
+            at = slice(d * rows, (d + 1) * rows)
+            both = dot_nn(ref[...], full[:, 4 * D :])
+            info = spot_col[at, :]
+            task = info[:, 32:33]
+            logits = jnp.where(task < 0.5, both, pltpu.roll(both, LANES - EXPERTS, 1))
+            chosen = pltpu.roll(info, LANES - 16, 1)
+            open_ = (lane < EXPERTS) & (chosen > 0.5)
+            logits = jnp.where(open_, logits, MASKED)
+            raised = jnp.where(open_, jnp.exp(logits - jnp.max(logits, axis=1, keepdims=True)), 0.0)
+            gates[at, :] = raised / jnp.sum(raised, axis=1, keepdims=True)
+
+    low_up[...] = up[0].astype(BF16)
+    low_down[...] = down[0].astype(BF16)
+    expert = base + step
+    slot_at = lax.broadcasted_iota(jnp.int32, (CAP, rows), 0).astype(F32)
+    slot_along = lax.broadcasted_iota(jnp.int32, (rows, CAP), 1).astype(F32)
+    mixes = (m0, m1, m2, m3)
+    grads = (g0, g1, g2, g3)
+    for d in range(4):
+        at = slice(d * rows, (d + 1) * rows)
+        spots = spot_row[pl.ds(step, 1), at]
+        pick = jnp.where(slot_at == spots, 1.0, 0.0).astype(BF16)
+        gate = jnp.sum(jnp.where(lane == expert, gates[at, :], 0.0), axis=1, keepdims=True)
+        scaled = (gate * grads[d][...].astype(F32)).astype(BF16)
+        start = pl.multiple_of(plan[step * 8 + d], 16)
+        hidden[pl.ds(start, CAP), :] = dot_nn(pick, mixes[d][...]).astype(BF16)
+        upstream[pl.ds(start, CAP), :] = dot_nn(pick, scaled).astype(BF16)
+    ending = pl.multiple_of(plan[step * 8 + 4], 16)
+    hidden[pl.ds(ending, CAP), :] = jnp.zeros((CAP, D), BF16)
+    upstream[pl.ds(ending, CAP), :] = jnp.zeros((CAP, D), BF16)
+    sum_up[...] = jnp.zeros_like(sum_up)
+    sum_down[...] = jnp.zeros_like(sum_down)
+    wide = 512
+
+    def tile(i, carry):
+        at = pl.ds(pl.multiple_of(i * CAP, CAP), CAP)
+        x = hidden[at, :]
+        g = upstream[at, :]
+        x_t = jnp.transpose(x)
+        g_t = jnp.transpose(g)
+        made = jnp.zeros((CAP, D), F32)
+        back = jnp.zeros((CAP, D), F32)
+        for j in range(FFN // wide):
+            cols = slice(j * wide, (j + 1) * wide)
+            pre = dot_nn(x, low_up[:, cols])
+            pull = dot_nt(g, low_down[cols, :])
+            share = 0.5 + 0.5 * lax.erf(pre * 0.7071067811865476)
+            active = (pre * share).astype(BF16)
+            slope = share + pre * (0.3989422804014327 * jnp.exp(-0.5 * pre * pre))
+            pre_grad = (slope * pull).astype(BF16)
+            made = made + dot_nn(active, low_down[cols, :])
+            back = back + dot_nt(pre_grad, low_up[:, cols])
+            sum_up[:, cols] += dot_nn(x_t, pre_grad)
+            sum_down[:, cols] += dot_nn(g_t, active)
+        results[at, :D] = made.astype(BF16)
+        results[at, D:] = back.astype(BF16)
+        return carry
+
+    lax.fori_loop(0, plan[step * 8 + 5], tile, 0)
+    for d in range(4):
+        at = slice(d * rows, (d + 1) * rows)
+        info = spot_col[at, :]
+        spots = jnp.sum(jnp.where(lane == step, info, 0.0), axis=1, keepdims=True)
+        put = jnp.where(slot_along == spots, 1.0, 0.0).astype(BF16)
+        start = pl.multiple_of(plan[step * 8 + d], 16)
+        got = dot_nn(put, results[pl.ds(start, CAP), :])
+        gate = jnp.sum(jnp.where(lane == expert, gates[at, :], 0.0), axis=1, keepdims=True)
+        out = got[:, :D]
+        gained = jnp.sum(grads[d][...].astype(F32) * out, axis=1, keepdims=True)
+        terms[at, :] = jnp.where(lane == expert, gate * gained, terms[at, :])
+        mix_acc[at, :] += gate * out
+        back_acc[at, :] += got[:, D:]
+    half = FFN // 2
+    for b in range(2):
+        for ref, side in ((mine, core), (other, 1 - core)):
+            cols = pl.ds(pl.multiple_of(side * half + b * D, LANES), D)
+            ref[0, b * D : (b + 1) * D, :] = sum_down[:, cols].astype(BF16)
+            ref[0, (2 + b) * D : (3 + b) * D, :] = sum_up[:, cols].astype(BF16)
+
+    @pl.when(step == last)
+    def _():
+        total = jnp.zeros((D, LANES), F32)
+        for d, ref in enumerate((m0, m1, m2, m3)):
+            at = slice(d * rows, (d + 1) * rows)
+            held = terms[at, :]
+            change = held - jnp.sum(held, axis=1, keepdims=True) * gates[at, :]
+            task = spot_col[at, 32:33]
+            first = jnp.where((lane < EXPERTS) & (task < 0.5), change, 0.0)
+            second = jnp.where(
+                (lane >= EXPERTS) & (lane < 2 * EXPERTS) & (task > 0.5), pltpu.roll(change, EXPERTS, 1), 0.0
+            )
+            both = first + second
+            high = both.astype(BF16)
+            low = (both - high.astype(F32)).astype(BF16)
+            routers = full[:, 4 * D :]
+            pulled = dot_nt(high, routers) + dot_nt(low, routers)
+            total = total + dot_tn(ref[...], high) + dot_tn(ref[...], low)
+            back_out[d] = (back_acc[at, :] + pulled).astype(BF16)
+            mix_out[d] = mix_acc[at, :].astype(BF16)
+        router_out[...] = total
+
+
+def expert_call(plan, meta, mixes, grads, spot_row, spot_col, full, up, down):
+    rows = mixes[0].shape[0]
+    count = up.shape[0]
+    slots = 4 * CAP + CAP
+
+    def whole(shape):
+        return pl.BlockSpec(shape, lambda e, *_: (0,) * len(shape), pipeline_mode=pl.Buffered(1))
+
+    return pl.pallas_call(
+        expert_kernel,
+        grid_spec=pltpu.PrefetchScalarGridSpec(
+            num_scalar_prefetch=2,
+            grid=(count,),
+            in_specs=[whole((rows, D))] * 8
+            + [
+                whole((8, 4 * rows)),
+                whole((4 * rows, LANES)),
+                whole((D, WCOLS)),
+                pl.BlockSpec((1, D, FFN), lambda e, *_: (e, 0, 0)),
+                pl.BlockSpec((1, FFN, D), lambda e, *_: (e, 0, 0)),
+            ],
+            out_specs=(
+                pl.BlockSpec((1, 4 * D, D), lambda e, *_: (e, 0, 0)),
+                pl.BlockSpec((1, 4 * D, D), lambda e, *_: (e, 0, 0)),
+                whole((4, rows, D)),
+                whole((4, rows, D)),
+                whole((D, LANES)),
+            ),
+            scratch_shapes=[
+                pltpu.VMEM((4 * rows, LANES), F32),
+                pltpu.VMEM((4 * rows, LANES), F32),
+                pltpu.VMEM((4 * rows, D), F32),
+                pltpu.VMEM((4 * rows, D), F32),
+                pltpu.VMEM((slots, D), BF16),
+                pltpu.VMEM((slots, D), BF16),
+                pltpu.VMEM((slots, 2 * D), BF16),
+                pltpu.VMEM((D, FFN), BF16),
+                pltpu.VMEM((FFN, D), BF16),
+                pltpu.VMEM((D, FFN), F32),
+                pltpu.VMEM((D, FFN), F32),
+            ],
+        ),
+        out_shape=(
+            jax.ShapeDtypeStruct((count, 4 * D, D), BF16),
+            jax.ShapeDtypeStruct((count, 4 * D, D), BF16),
+            jax.ShapeDtypeStruct((4, rows, D), BF16),
+            jax.ShapeDtypeStruct((4, rows, D), BF16),
+            jax.ShapeDtypeStruct((D, LANES), F32),
+        ),
+        name="experts",
+    )(plan, meta, *mixes, *grads, spot_row, spot_col, full, up, down)
+
+
+def turn_kernel(b0, r1, r2, r3, middle, grad, full, att, lse_row, middle_grad, sent, dots_col, output_grad, norm_two):
+    rows = middle.shape[0]
+    norms = norm_rows_of(full)
+    mixed_grad = b0[0].astype(F32) + r1[...].astype(F32) + r2[...].astype(F32) + r3[...].astype(F32)
+    unit, scale = unit_rows(middle[...])
+    norm_two[...] = jnp.zeros_like(norm_two)
+    norm_two[0:1, :] = jnp.sum(mixed_grad * unit, axis=0, keepdims=True)
+    norm_two[1:2, :] = jnp.sum(mixed_grad, axis=0, keepdims=True)
+    pulled = mixed_grad * norms[2:3]
+    through = pulled - jnp.mean(pulled, axis=1, keepdims=True)
+    through = scale * (through - unit * jnp.mean(pulled * unit, axis=1, keepdims=True))
+    whole = through + grad[...].astype(F32)
+    middle_grad[...] = whole
+    branch = whole.astype(BF16)
+    output_grad[...] = dot_tn(att[...].astype(BF16), branch).astype(BF16)
+    pulled = dot_nt(branch, full[:, 3 * D : 4 * D]).astype(BF16)
+    sent[0:rows, :] = pulled
+    product = pulled.astype(F32) * att[...]
+    high = product.astype(BF16)
+    low = (product - high.astype(F32)).astype(BF16)
+    heads = (
+        lax.broadcasted_iota(jnp.int32, (D, LANES), 0) // HEAD_DIM
+        == lax.broadcasted_iota(jnp.int32, (D, LANES), 1)
+    )
+    heads = heads.astype(F32).astype(BF16)
+    dots = dot_nn(high, heads) + dot_nn(low, heads)
+    dots_col[...] = dots
+    lines = jnp.concatenate([lse_row[...], jnp.transpose(dots)[:8]], axis=0)
+    high = lines.astype(BF16).astype(F32)
+    table = jnp.concatenate([high, lines - high], axis=0).astype(BF16)
+    half = EXTRA // 2
+    sent[rows : rows + half, :] = table[:, :D]
+    sent[rows + half : rows + EXTRA, :] = jnp.zeros((half, D), BF16)
+    sent[rows + half : rows + EXTRA, : rows - D] = table[:, D:]
+
+
+def turn_call(back, received, middle, grad, full, att, lse_row):
+    rows = middle.shape[0]
+    return pl.pallas_call(
+        turn_kernel,
+        grid=(1,),
+        in_specs=[pl.BlockSpec((1, rows, D), lambda i: (0, 0, 0))] + [vmem()] * 8,
+        out_specs=(vmem(),) * 5,
+        out_shape=(
+            jax.ShapeDtypeStruct((rows, D), F32),
+            jax.ShapeDtypeStruct((rows + EXTRA, D), BF16),
+            jax.ShapeDtypeStruct((rows, LANES), F32),
+            jax.ShapeDtypeStruct((D, D), BF16),
+            jax.ShapeDtypeStruct((8, D), F32),
+        ),
+        name="turn",
+    )(back, *received, middle, grad, full, att, lse_row)
+
+
+def attention_back_kernel(
+    meta, image, qkv, s0, s1, s2, s3, lse_col, dots_col, own, full, middle_grad, output_grad, norm_two, routers,
+    input_grad, shared,
+    lines, grads, packed, acc_one, acc_two,
+):
+    rows = input_grad.shape[0]
+    half_extra = EXTRA // 2
+    for d, ref in enumerate((s0, s1, s2, s3)):
+        grads[d] = ref[0:rows, :]
+        table = jnp.concatenate(
+            [ref[rows : rows + half_extra, :], ref[rows + half_extra : rows + EXTRA, : rows - D]], axis=1
+        ).astype(F32)
+        lines[d] = table[:16] + table[16:]
+    own_row = image[pl.ds(meta[4], 1), :].astype(F32)
+    own_col = jnp.transpose(jnp.broadcast_to(own_row, (LANES, rows)))[:, :1]
+    lane = lax.broadcasted_iota(jnp.int32, (rows, LANES), 1)
+    none = jnp.zeros((), BF16)
+    here = slice(0, rows)
+
+    def pair_of_heads(pair, carry):
+        lanes = pl.ds(pl.multiple_of(pair * LANES, LANES), LANES)
+        made = []
+        for half in range(2):
+            head = 2 * pair + half
+            held = (lane < HEAD_DIM) if half == 0 else (lane >= HEAD_DIM)
+            query = jnp.where(held, qkv[pair, here, :], none)
+            pull = jnp.where(held, grads[0, :, lanes], none)
+            log_total = jnp.sum(jnp.where(lane == head, lse_col[...], 0.0), axis=1, keepdims=True)
+            dots = jnp.sum(jnp.where(lane == head, dots_col[...], 0.0), axis=1, keepdims=True)
+            acc_one[...] = jnp.zeros_like(acc_one)
+
+            def over_keys(d, c):
+                @pl.when(meta[8 + d] > 0)
+                def _():
+                    at = pl.ds(pl.multiple_of(d * rows, rows), rows)
+                    key = qkv[PAIRS + pair, at, :]
+                    same = own_col == image[pl.ds(meta[4 + d], 1), :].astype(F32)
+                    shares = jnp.where(same, jnp.exp(dot_nt(query, key) - log_total), 0.0)
+                    change = dot_nt(pull, qkv[2 * PAIRS + pair, at, :]) - dots
+                    acc_one[...] += dot_nn((shares * change).astype(BF16), key)
+
+                return c
+
+            lax.fori_loop(0, 4, over_keys, 0)
+            made.append(acc_one[...])
+        packed[:, lanes] = jnp.where(lane < HEAD_DIM, made[0], made[1]) * (HEAD_DIM ** (-0.5))
+        made = []
+        for half in range(2):
+            head = 2 * pair + half
+            held = (lane < HEAD_DIM) if half == 0 else (lane >= HEAD_DIM)
+            key = jnp.where(held, qkv[PAIRS + pair, here, :], none)
+            value = jnp.where(held, qkv[2 * PAIRS + pair, here, :], none)
+            acc_one[...] = jnp.zeros_like(acc_one)
+            acc_two[...] = jnp.zeros_like(acc_two)
+
+            def over_queries(d, c):
+                @pl.when(meta[8 + d] > 0)
+                def _():
+                    at = pl.ds(pl.multiple_of(d * rows, rows), rows)
+                    query = qkv[pair, at, :]
+                    pull = grads[d, :, lanes]
+                    same = own_col == image[pl.ds(meta[4 + d], 1), :].astype(F32)
+                    log_total = lines[d, pl.ds(head, 1), :]
+                    dots = lines[d, pl.ds(8 + head, 1), :]
+                    shares = jnp.where(same, jnp.exp(dot_nt(key, query) - log_total), 0.0)
+                    change = dot_nt(value, pull) - dots
+                    acc_two[...] += dot_nn(shares.astype(BF16), pull)
+                    acc_one[...] += dot_nn((shares * change).astype(BF16), query)
+
+                return c
+
+            lax.fori_loop(0, 4, over_queries, 0)
+            made.append((acc_one[...], acc_two[...]))
+        shift = pl.ds(pl.multiple_of(D + pair * LANES, LANES), LANES)
+        packed[:, shift] = jnp.where(lane < HEAD_DIM, made[0][0], made[1][0])
+        shift = pl.ds(pl.multiple_of(2 * D + pair * LANES, LANES), LANES)
+        packed[:, shift] = jnp.where(lane < HEAD_DIM, made[0][1], made[1][1])
+        return carry
+
+    lax.fori_loop(0, PAIRS, pair_of_heads, 0)
+    norms = norm_rows_of(full)
+    unit, scale = unit_rows(own[0:rows, :].astype(F32))
+    normed = (unit * norms[0:1] + norms[1:2]).astype(BF16)
+    normed_grad = jnp.zeros((rows, D), F32)
+    for third in range(3):
+        part = packed[:, third * D : (third + 1) * D].astype(BF16)
+        normed_grad = normed_grad + dot_nt(part, full[:, third * D : (third + 1) * D])
+        weight_grad = dot_tn(normed, part).astype(BF16)
+        for j in range(PAIRS):
+            block = third * PAIRS + j
+            shared[meta[24 + block // 4], :, block % 4 * LANES : (block % 4 + 1) * LANES] = weight_grad[
+                :, j * LANES : (j + 1) * LANES
+            ]
+    pulled = normed_grad * norms[0:1]
+    through = pulled - jnp.mean(pulled, axis=1, keepdims=True)
+    through = scale * (through - unit * jnp.mean(pulled * unit, axis=1, keepdims=True))
+    input_grad[...] = through + middle_grad[...]
+    for j in range(PAIRS):
+        block = 3 * PAIRS + j
+        shared[meta[24 + block // 4], :, block % 4 * LANES : (block % 4 + 1) * LANES] = output_grad[
+            :, j * LANES : (j + 1) * LANES
+        ]
+    lines_norm = jnp.concatenate(
+        [
+            jnp.zeros((NORM_AT, D), F32),
+            jnp.sum(normed_grad * unit, axis=0, keepdims=True),
+            jnp.sum(normed_grad, axis=0, keepdims=True),
+            norm_two[0:2, :],
+            jnp.zeros((LANES - NORM_AT - 4, D), F32),
+        ],
+        axis=0,
+    )
+    small = routers[...] + jnp.transpose(lines_norm)
+    shared[meta[27], :, 0:LANES] = small.astype(BF16)
+    shared[meta[27], :, LANES:] = jnp.zeros((D, 3 * LANES), BF16)
+
+
+def attention_back_call(meta, image, qkv, sent, lse_col, dots_col, own, full, middle_grad, output_grad, norm_two, routers):
+    rows = middle_grad.shape[0]
+    return pl.pallas_call(
+        attention_back_kernel,
+        in_specs=[smem()] + [vmem()] * 14,
+        out_specs=(vmem(),) * 2,
+        out_shape=(
+            jax.ShapeDtypeStruct((rows, D), F32),
+            jax.ShapeDtypeStruct((4, D, 4 * LANES), BF16),
+        ),
+        scratch_shapes=[
+            pltpu.VMEM((4, 16, rows), F32),
+            pltpu.VMEM((4, rows, D), BF16),
+            pltpu.VMEM((rows, 3 * D), F32),
+            pltpu.VMEM((rows, LANES), F32),
+            pltpu.VMEM((rows, LANES), F32),
+        ],
+        name="attention_back",
+    )(meta, image, qkv, *sent, lse_col, dots_col, own, full, middle_grad, output_grad, norm_two, routers)
 
 
 def adamw(weight, moment, second, gradient, step_rate):
@@ -45,6 +621,185 @@
     second_hat = second / (1.0 - BETA_SECOND**STEP)
     weight = weight - step_rate * (first_hat / (jnp.sqrt(second_hat) + ADAM_EPS) + DECAY * weight)
     return (weight, moment, second)
+
+
+def adam_kernel(meta, ready, passed, ready_two, passed_two, w1, m1, v1, w2, m2, v2, *rest):
+    outs = rest[-6:]
+    mine = (pl.program_id(0) // (FFN // 2 // LANES)) == meta[1]
+    down = jnp.where(mine, ready[...], passed[...]).astype(F32)
+    up = jnp.where(mine, ready_two[...], passed_two[...]).astype(F32)
+    for k, value in enumerate(adamw(w1[0], m1[0], v1[0], up, RATE_EXPAND)):
+        outs[k][0] = value
+    for k, value in enumerate(adamw(w2[0], m2[0], v2[0], jnp.transpose(down), RATE_REDUCE)):
+        outs[3 + k][0] = value
+
+
+def adam_call(expert, meta, ready, passed, states, previous):
+    steps = FFN // LANES
+    per = D // LANES
+
+    def part(first):
+        return pl.BlockSpec((D, LANES), lambda i, *_: (first + i // per % 2, i % per))
+
+    up = pl.BlockSpec((1, D, LANES), lambda i, *_: (expert, 0, i))
+    down = pl.BlockSpec((1, LANES, D), lambda i, *_: (expert, i, 0))
+    specs = [part(0), part(0), part(2), part(2)] + [up] * 3 + [down] * 3
+    args = [ready, passed, ready, passed, *states]
+    aliases = {}
+    if previous is not None:
+        for k, value in enumerate(previous):
+            aliases[1 + len(args)] = k
+            args.append(value)
+            specs.append(pl.BlockSpec(memory_space=pl.ANY))
+    return pl.pallas_call(
+        adam_kernel,
+        grid_spec=pltpu.PrefetchScalarGridSpec(
+            num_scalar_prefetch=1,
+            grid=(steps,),
+            in_specs=specs,
+            out_specs=(up,) * 3 + (down,) * 3,
+        ),
+        out_shape=tuple(jax.ShapeDtypeStruct(s.shape, F32) for s in states),
+        input_output_aliases=aliases,
+        name="adam",
+    )(meta, *args)
+
+
+def swap_expert(value, d):
+    return lax.ppermute(value, "expert", [(i, i ^ d) for i in range(4)])
+
+
+def swap_tall(value, d):
+    return lax.ppermute(value, "dp", [(2 * a + c, 2 * (a ^ d) + c) for a in range(4) for c in range(2)])
+
+
+def swap_core(value):
+    return lax.ppermute(value, "dp", [(i, i ^ 1) for i in range(8)])
+
+
+def send_tall(value, hops):
+    return lax.ppermute(value, "dp", [(2 * a + c, 2 * b + c) for a, b in hops for c in range(2)])
+
+
+def reduce_line(mine, other, inner):
+    half = mine + swap_core(other)
+    pair = half + send_tall(half, ((0, 1), (3, 2)))
+    whole = pair + send_tall(pair, ((1, 2), (2, 1)))
+    returned = send_tall(whole, ((1, 0), (2, 3)))
+    ready = jnp.where(inner, whole, returned)
+    return ready, swap_core(ready)
+
+
+def fast_body(
+    patches, out_grad, image_of, task_of, routes,
+    norm_weight, norm_moment, norm_second,
+    attend_weight, attend_moment, attend_second,
+    output_weight, output_moment, output_second,
+    router_weight, router_moment, router_second,
+    expand_weight, expand_moment, expand_second,
+    reduce_weight, reduce_moment, reduce_second,
+):
+    member = lax.axis_index("expert")
+    place = lax.axis_index("dp")
+    tall, core = place // 2, place % 2
+    rows = patches.shape[1]
+    count = expand_weight.shape[0]
+    shard_rows = attend_weight.shape[0]
+
+    lists = jnp.concatenate([routes[0].T, task_of], axis=0).astype(BF16)
+    lists = jnp.stack([lists[:, :D], jnp.pad(lists[:, D:], ((0, 0), (0, 2 * D - rows)))], axis=1)
+    lists = jnp.pad(lists.reshape(2 * (TOP + TASKS - 1), D), ((0, INFO - 2 * (TOP + TASKS - 1)), (0, 0)))
+    own = jnp.concatenate([patches[0], lists], axis=0)
+    pieces = [own] + [swap_expert(own, d) for d in (1, 2, 3)]
+    shard = jnp.concatenate(
+        [
+            attend_weight.astype(BF16),
+            output_weight.astype(BF16),
+            router_weight.reshape(TASKS * EXPERTS, shard_rows).T.astype(BF16),
+            norm_weight.T.astype(BF16),
+            jnp.zeros((shard_rows, LANES - NORM_AT - 4), BF16),
+        ],
+        axis=1,
+    )
+    shards = [shard] + [swap_tall(shard, d) for d in (1, 2, 3)]
+    shards = shards + [swap_core(s) for s in shards]
+    grad = out_grad[0]
+    grads = [grad] + [swap_expert(grad, d) for d in (1, 2, 3)]
+
+    image = image_of.reshape(4, rows)
+    order = [member ^ d for d in range(4)]
+    opens, closes = image[:, 0], image[:, rows - 1]
+    first, final = opens[member], closes[member]
+    needed = [((opens[o] <= final) & (closes[o] >= first)).astype(jnp.int32) for o in order]
+    spots = [shard_rows * (2 * (tall ^ d) + core) for d in range(4)]
+    spots = spots + [shard_rows * (2 * (tall ^ d) + 1 - core) for d in range(4)]
+    zero = jnp.int32(0)
+    meta = jnp.stack(
+        [member * count, core, zero, zero] + order + needed + [zero] * 4 + spots + order
+    ).astype(jnp.int32)
+
+    spot_row, spot_col, plan = route_call(meta, pieces, count)
+    qkv, full, att, lse_col, lse_row, middle, mixed = front_call(meta, image, pieces, shards)
+    mixes = [mixed] + [swap_expert(mixed, d) for d in (1, 2, 3)]
+    mine, other, back, mix, routers = expert_call(
+        plan, meta, mixes, grads, spot_row, spot_col, full, expand_weight, reduce_weight
+    )
+    inner = (tall == 1) | (tall == 2)
+    returned = [swap_expert(back[d], d) for d in (1, 2, 3)]
+    middle_grad, sent, dots_col, output_grad, norm_two = turn_call(
+        back, returned, middle, grad, full, att, lse_row
+    )
+    sents = [sent] + [swap_expert(sent, d) for d in (1, 2, 3)]
+    input_grad, shared = attention_back_call(
+        meta, image, qkv, sents, lse_col, dots_col, own, full, middle_grad, output_grad, norm_two, routers
+    )
+    states = (expand_weight, expand_moment, expand_second, reduce_weight, reduce_moment, reduce_second)
+    news = None
+    for e in range(count):
+        ready, passed = reduce_line(mine[e], other[e], inner)
+        news = adam_call(e, meta, ready, passed, states, news)
+    parts = [swap_expert(mix[d], d) for d in (1, 2, 3)]
+    block_out = middle + mix[0].astype(F32)
+    for part in parts:
+        block_out = block_out + part.astype(F32)
+    block_out = block_out.astype(BF16)[None]
+
+    quarter = shared[0].astype(F32)
+    for d in (1, 2, 3):
+        quarter = quarter + swap_expert(shared[d], d).astype(F32)
+    quarter = quarter.astype(BF16).reshape(4, 2, shard_rows, 4 * LANES)
+    kept = lax.dynamic_index_in_dim(quarter, core, 1, False)
+    gone = lax.dynamic_index_in_dim(quarter, 1 - core, 1, False)
+    kept = kept + swap_core(gone)
+    piece = lax.dynamic_index_in_dim(kept, tall, 0, False).astype(F32)
+    for d in (1, 2, 3):
+        piece = piece + swap_tall(lax.dynamic_index_in_dim(kept, tall ^ d, 0, False), d).astype(F32)
+    piece = piece.astype(BF16)
+    quarters = jnp.stack([piece] + [swap_expert(piece, d) for d in (1, 2, 3)])
+    quarters = jnp.concatenate([quarters[o] for o in order], axis=1).astype(F32)
+    attend_sum = quarters[:, : 3 * D]
+    output_sum = quarters[:, 3 * D : 4 * D]
+    router_sum = quarters[:, 4 * D : 4 * D + NORM_AT].T.reshape(router_weight.shape)
+    norm_sum = quarters[:, 4 * D + NORM_AT : 4 * D + NORM_AT + 4].T
+    norm_new = adamw(norm_weight, norm_moment, norm_second, norm_sum, RATE_NORM)
+    attend_new = adamw(attend_weight, attend_moment, attend_second, attend_sum, RATE_ATTEND)
+    output_new = adamw(output_weight, output_moment, output_second, output_sum, RATE_OUTPUT)
+    router_new = adamw(router_weight, router_moment, router_second, router_sum, RATE_ROUTER)
+    return (
+        block_out, input_grad[None],
+        *norm_new, *attend_new, *output_new, *router_new, *news,
+    )
+
+
+def gelu_exact(values):
+    return 0.5 * values * (1.0 + lax.erf(values * 0.7071067811865476))
+
+
+def norm_rows(values, gain_row, offset):
+    average = jnp.mean(values, axis=-1, keepdims=True)
+    centred = values - average
+    spread = jnp.mean(centred * centred, axis=-1, keepdims=True)
+    return centred * lax.rsqrt(spread + NORM_EPS) * gain_row + offset
 
 
 def body(
@@ -390,8 +1145,9 @@
         P("expert", None, None),
         P("expert", None, None),
     )
+    fits = mesh.shape["dp"] == 8 and mesh.shape["expert"] == 4
     return jax.shard_map(
-        body,
+        fast_body if fits else body,
         mesh=mesh,
         in_specs=placed,
         out_specs=(

time: 889 us -> 553 us (0.62)
  Pallas kernels: 0 us -> 179 us
  waiting for transfers between devices: 322 us -> 144 us
  blocking collectives: 173 us -> 0 us
  matrix products: 138 us -> 0 us
  starting transfers between devices: 8.15 us -> 126 us
  local copies, waits for them, and re-layouts: 116 us -> 34.2 us
  other arithmetic: 108 us -> 46 us
    psum x2 -> x0, waiting for transfers between devices: 232 us -> none  [the longest x1 190 us: body(): lax.psum(expand_grad.astype(jnp.bfloat16), 'dp').astype(jnp.float32)]
    pallas_call x0 -> x9, Pallas kernels: none -> 179 us  [the longest x4 67.7 us: adam_call(): pl.pallas_call(adam_kernel, grid_spec=pltpu.PrefetchScalarGridSpec(num_sc...]
    ppermute x0 -> x55, waiting for transfers between devices: none -> 144 us  [the longest x24 64.9 us: swap_expert(): return lax.ppermute(value, 'expert', [(i, i ^ d) for i in range(4)])]
    dot_general x32 -> x0, matrix products: 138 us -> none  [the longest x1 21.4 us: body(): jnp.einsum('ecd,ehd->ech', grad_in, reduce_low, preferred_element_type=jn...]
    ppermute x0 -> x55, starting transfers between devices: none -> 126 us  [the longest x6 36.7 us: swap_tall(): lax.ppermute(value, 'dp', [(2 * a + c, 2 * (a ^ d) + c) for a in range(4)...]
    all_gather x4 -> x0, blocking collectives: 83.7 us -> none  [the longest x1 38.8 us: body(): lax.all_gather(router_weight.astype(jnp.bfloat16), 'dp', axis=2, tiled=True)]
    all_to_all x2 -> x0, blocking collectives: 72.2 us -> none  [the longest x1 41.8 us: body(): lax.all_to_all(scatter_pairs(pair_grad), 'expert', split_axis=0, concat_a...]
    reduce_scatter x3 -> x0, waiting for transfers between devices: 62.6 us -> none  [the longest x1 35.8 us: body(): lax.psum_scatter(key_value_terms.astype(jnp.bfloat16), 'expert', scatter_...]
  transfers between devices with their start and end apart: 10 -> 55, of which waited for: 7 -> 23; matrix products, arithmetic and copies ran while one was open for 23% -> 12% of each run, Pallas kernels for 0% -> 20%
where the time goes in v1:
time: 553 us; the launch traced here: 542 us
  Pallas kernels  179 us (32%)
  waiting for transfers between devices  144 us (26%)
  starting transfers between devices  126 us (23%)
  other arithmetic  46 us (8%)
  local copies, waits for them, and re-layouts  34.2 us (6%)
  between operations  12.3 us (2%)
    pallas_call x4, Pallas kernels, adam_call(): pl.pallas_call(adam_kernel, grid_spec=pltpu.PrefetchScalarGridSpec(num_sc...  67.7 us
    ppermute x24, waiting for transfers between devices, swap_expert(): return lax.ppermute(value, 'expert', [(i, i ^ d) for i in range(4)])  64.9 us
    pallas_call x1, Pallas kernels, expert_call(): pl.pallas_call(expert_kernel, grid_spec=pltpu.PrefetchScalarGridSpec(num_...  54.1 us
    ppermute x12, waiting for transfers between devices, send_tall(): lax.ppermute(value, 'dp', [(2 * a + c, 2 * b + c) for a, b in hops for c...  54 us
    ppermute x6, starting transfers between devices, swap_tall(): lax.ppermute(value, 'dp', [(2 * a + c, 2 * (a ^ d) + c) for a in range(4)...  36.7 us
    ppermute x24, starting transfers between devices, swap_expert(): return lax.ppermute(value, 'expert', [(i, i ^ d) for i in range(4)])  35.8 us
    ppermute x13, starting transfers between devices, swap_core(): return lax.ppermute(value, 'dp', [(i, i ^ 1) for i in range(8)])  28 us
    pallas_call x1, Pallas kernels, attention_back_call(): pl.pallas_call(attention_back_kernel, in_specs=[smem()] + [vmem()] * 14,...  26.7 us
  transfers between devices with their start and end apart: 55, of which 23 were waited for; matrix products, arithmetic and copies ran while one was open for 12% of the time, Pallas kernels for 20%

profile of v1, /device:TPU:0, one launch (start us, length us, event | category | flops | bytes accessed | tf_op | source)
XLA Modules:
  0.0 542.3 jit_solution(9974386922144731850)
XLA Ops:
  4.9 4.7 collective-permute-start.5
  11.6 3.1 collective-permute-done.5.w3
  14.8 2.7 collective-permute-start.2
  18.0 5.7 %collective-permute-done.4.w2 = bf16[48,1664]{1,0:T(8,128)(2,1)S(1)} collective-permute-done((bf16[48,1664]{1,0:T(8,128)(2,1)S(1)}, bf16[48,1664]{1,0:T(8,128)(2,1)S(1)}, u32[]{:S(2)}, u32[]{:S(2)}) %collective-permute-start.4) | collective-permute-done | bytes 159776 | tf_op jit(solution)/shard_map/ppermute | solution.py:673
  43.9 22.7 %front.1 = (bf16[9,2048,128]{2,1,0:T(8,128)(2,1)}, bf16[384,1664]{1,0:T(8,128)(2,1)}, f32[512,384]{1,0:T(8,128)}, f32[512,128]{1,0:T(8,128)}, f32[8,512]{1,0:T(8...) custom-call(s32[28]{0:T(128)} %stack.119.meta, s32[4,512]{1,0:T(4,128)} %copy-done.40, bf16[528,384]{1,0:T(8,128)(2,1)} %copy-done.3, ...), custom_call_target="tpu_custom_call" | custom-call | tf_op jit(solution)/shard_map/front/pallas_call | solution.py:226
  70.2 2.9 routing.1
  73.1 4.6 collective-permute-done.12.m3
  77.7 10.0 %collective-permute-done.11.m2 = bf16[512,384]{1,0:T(8,128)(2,1)S(1)} collective-permute-done((bf16[512,384]{1,0:T(8,128)(2,1)}, bf16[512,384]{1,0:T(8,128)(2,1)S(1)}, u32[]{:S(2)}, u32[]{:S(2)}) %collective-permute-start.11) | collective-permute-done | bytes 393248 | tf_op jit(solution)/shard_map/ppermute | solution.py:669
  88.7 54.1 %experts.1 = (bf16[4,1536,384]{2,1,0:T(8,128)(2,1)}, bf16[4,1536,384]{2,1,0:T(8,128)(2,1)}, bf16[4,512,384]{2,1,0:T(8,128)(2,1)}, bf16[4,512,384]{2,1,0:T(8,128)(2,1)}, f32[384,128]{1,0:T(8,128)}) custom-call(s32[32]{0:T(128)} %get-tuple-element.67.plan, s32[28]{0:T(128)} %stack.119.meta, bf16[512,384]{1,0:T(8,128)(2,1)} %get-tuple-element.68.m0, ...), custom_call_target="tpu_custom_call" | custom-call | tf_op jit(solution)/shard_map/experts/pallas_call | solution.py:380
  142.8 3.0 slice_bitcast_fusion
  146.9 1.8 collective-permute-done.50
  148.7 1.7 collective-permute-done.45
  152.1 1.7 collective-permute-done.35
  153.8 1.9 bitcast_add_fusion
  155.7 2.3 collective-permute-start.51
  158.2 7.0 %collective-permute-start.21 = (bf16[512,384]{1,0:T(8,128)(2,1)S(1)}, bf16[512,384]{1,0:T(8,128)(2,1)S(1)}, u32[]{:S(2)}, u32[]{:S(2)}) collective-permute-start(bf16[512,384]{1,0:T(8,128)(2,1)S(1)} %get-tuple-element.235), channel_id=1, source_target_pairs={{0,3},{1,2},{2,1},{3,0},{4,7},{5,6},{6,5},{7,4},{8,11},{9,10},{10,... | collective-permute-start | bytes 1179656 | tf_op jit(solution)/shard_map/ppermute | solution.py:669
  165.8 9.4 %collective-permute-done.21.r3 = bf16[512,384]{1,0:T(8,128)(2,1)S(1)} collective-permute-done((bf16[512,384]{1,0:T(8,128)(2,1)S(1)}, bf16[512,384]{1,0:T(8,128)(2,1)S(1)}, u32[]{:S(2)}, u32[]{:S(2)}) %collective-permute-start.21) | collective-permute-done | bytes 393248 | tf_op jit(solution)/shard_map/ppermute | solution.py:669
  175.2 7.5 %collective-permute-done.20.r2 = bf16[512,384]{1,0:T(8,128)(2,1)S(1)} collective-permute-done((bf16[512,384]{1,0:T(8,128)(2,1)S(1)}, bf16[512,384]{1,0:T(8,128)(2,1)S(1)}, u32[]{:S(2)}, u32[]{:S(2)}) %collective-permute-start.20) | collective-permute-done | bytes 393248 | tf_op jit(solution)/shard_map/ppermute | solution.py:669
  183.6 4.9 turn.1
  188.5 1.8 collective-permute-start.24
  192.0 2.7 collective-permute-start.46
  194.7 8.0 %collective-permute-done.24.s3 = bf16[576,384]{1,0:T(8,128)(2,1)S(1)} collective-permute-done((bf16[576,384]{1,0:T(8,128)(2,1)}, bf16[576,384]{1,0:T(8,128)(2,1)S(1)}, u32[]{:S(2)}, u32[]{:S(2)}) %collective-permute-start.24) | collective-permute-done | bytes 442400 | tf_op jit(solution)/shard_map/ppermute | solution.py:669
  202.7 8.3 %collective-permute-done.23.s2 = bf16[576,384]{1,0:T(8,128)(2,1)S(1)} collective-permute-done((bf16[576,384]{1,0:T(8,128)(2,1)}, bf16[576,384]{1,0:T(8,128)(2,1)S(1)}, u32[]{:S(2)}, u32[]{:S(2)}) %collective-permute-start.23) | collective-permute-done | bytes 442400 | tf_op jit(solution)/shard_map/ppermute | solution.py:669
  211.9 26.7 %attention_back.1 = (f32[512,384]{1,0:T(8,128)}, bf16[4,384,512]{2,1,0:T(8,128)(2,1)}) custom-call(s32[28]{0:T(128)} %stack.119.meta, s32[4,512]{1,0:T(4,128)} %copy-done.40, bf16[9,2048,128]{2,1,0:T(8,128)(2,1)} %get-tuple-element.73.qkv, bf16[576,384]{1,0:T(8,128)(2,1)} %get-tuple-element.77.s0, bf16[576,384]{1,0:T(8,128)(2,1)} %copy-done.22, ...), custom_call_target="tpu_custom_call" | custom-call | tf_op jit(solution)/shard_map/attention_back/pallas_call | solution.py:598
  238.6 2.8 collective-permute-start.41
  241.4 2.3 slice_bitcast_fusion.6
  247.1 2.6 add.265
  249.7 2.0 collective-permute-done.25
  251.7 5.6 %collective-permute-start.36 = (bf16[1536,384]{1,0:T(8,128)(2,1)S(1)}, bf16[1536,384]{1,0:T(8,128)(2,1)}, u32[]{:S(2)}, u32[]{:S(2)}) collective-permute-start(bf16[1536,384]{1,0:T(8,128)(2,1)S(1)} %get-tuple-element.227), channel_id=1, source_target_pairs={{0,8},{4,12},{24,16},{28,20},{1,9},{5,13},{25,17},{29,21},{2,10},{... | collective-permute-start | bytes 3538952 | tf_op jit(solution)/shard_map/ppermute | solution.py:681
  261.5 11.5 %collective-permute-start.28 = (bf16[4,48,512]{2,1,0:T(8,128)(2,1)S(1)}, bf16[4,48,512]{2,1,0:T(8,128)(2,1)S(1)}, u32[]{:S(2)}, u32[]{:S(2)}) collective-permute-start(bf16[4,48,512]{2,1,0:T(8,128)(2,1)S(1)} %dynamic-slice_bitcast_fusion), channel_id=1, source_target_pairs={{0,4},{4,0},{8,12},{12,8},{16,20},{20,16},{24,28},{28,24},{1,5},{5... | collective-permute-start | bytes 589832 | tf_op jit(solution)/shard_map/ppermute | solution.py:677
  273.0 2.9 add.262
  275.9 1.7 collective-permute-start.47
  279.8 2.0 collective-permute-start.18
  281.9 2.6 add.259
  284.5 6.5 %collective-permute-done.16 = bf16[512,384]{1,0:T(8,128)(2,1)} collective-permute-done((bf16[512,384]{1,0:T(8,128)(2,1)}, bf16[512,384]{1,0:T(8,128)(2,1)}, u32[]{:S(2)}, u32[]{:S(2)}) %collective-permute-start.16) | collective-permute-done | bytes 393248 | tf_op jit(solution)/shard_map/ppermute | solution.py:669
  290.9 1.7 collective-permute-start.42
  292.7 7.1 %collective-permute-done.18 = bf16[512,384]{1,0:T(8,128)(2,1)} collective-permute-done((bf16[512,384]{1,0:T(8,128)(2,1)}, bf16[512,384]{1,0:T(8,128)(2,1)}, u32[]{:S(2)}, u32[]{:S(2)}) %collective-permute-start.18) | collective-permute-done | bytes 393248 | tf_op jit(solution)/shard_map/ppermute | solution.py:669
  299.7 4.1 collective-permute-done.29
  304.2 5.6 %collective-permute-done.31 = bf16[48,512]{1,0:T(8,128)(2,1)S(1)} collective-permute-done((bf16[48,512]{1,0:T(8,128)(2,1)S(1)}, bf16[48,512]{1,0:T(8,128)(2,1)S(1)}, u32[]{:S(2)}, u32[]{:S(2)}) %collective-permute-start.31) | collective-permute-done | bytes 49184 | tf_op jit(solution)/shard_map/ppermute | solution.py:673
  309.8 31.0 %collective-permute-start.30 = (bf16[48,512]{1,0:T(8,128)(2,1)S(1)}, bf16[48,512]{1,0:T(8,128)(2,1)S(1)}, u32[]{:S(2)}, u32[]{:S(2)}) collective-permute-start(bf16[48,512]{1,0:T(8,128)(2,1)S(1)} %get-tuple-element.247), channel_id=1, source_target_pairs={{0,16},{4,20},{8,24},{12,28},{16,0},{20,4},{24,8},{28,12},{1,17},{... | collective-permute-start | bytes 147464 | tf_op jit(solution)/shard_map/ppermute | solution.py:673
  344.1 1.8 collective-permute-start.37
  346.0 1.9 add.266
  351.6 2.8 collective-permute-start.34
  359.4 2.0 copy.141
  362.5 2.0 add.263
  365.9 2.4 fusion.10
  369.8 2.9 add.260
  374.7 1.9 copy.140
  377.8 1.9 add.257
  381.2 2.5 broadcast_select_fusion.ready.ready_two
  384.9 17.1 %collective-permute-done.48 = bf16[1536,384]{1,0:T(8,128)(2,1)} collective-permute-done((bf16[1536,384]{1,0:T(8,128)(2,1)S(1)}, bf16[1536,384]{1,0:T(8,128)(2,1)}, u32[]{:S(2)}, u32[]{:S(2)}) %collective-permute-start.48) | collective-permute-done | bytes 1179680 | tf_op jit(solution)/shard_map/ppermute | solution.py:681
  403.5 5.4 %collective-permute-start.49 = (bf16[1536,384]{1,0:T(8,128)(2,1)S(1)}, bf16[1536,384]{1,0:T(8,128)(2,1)}, u32[]{:S(2)}, u32[]{:S(2)}) collective-permute-start(bf16[1536,384]{1,0:T(8,128)(2,1)S(1)} %broadcast_select_fusion.1.ready.ready_two), channel_id=1, source_target_pairs={{0,4},{4,0},{8,12},{12,8},{16,20},{20,16},{24,28},{28,24},{1,5},{5... | collective-permute-start | bytes 3538952 | tf_op jit(solution)/shard_map/ppermute | solution.py:677
  408.9 18.4 %collective-permute-done.43 = bf16[1536,384]{1,0:T(8,128)(2,1)} collective-permute-done((bf16[1536,384]{1,0:T(8,128)(2,1)}, bf16[1536,384]{1,0:T(8,128)(2,1)}, u32[]{:S(2)}, u32[]{:S(2)}) %collective-permute-start.43) | collective-permute-done | bytes 1179680 | tf_op jit(solution)/shard_map/ppermute | solution.py:681
  428.8 5.3 collective-permute-start.44
  434.1 18.4 %collective-permute-done.38 = bf16[1536,384]{1,0:T(8,128)(2,1)S(1)} collective-permute-done((bf16[1536,384]{1,0:T(8,128)(2,1)S(1)}, bf16[1536,384]{1,0:T(8,128)(2,1)S(1)}, u32[]{:S(2)}, u32[]{:S(2)}) %collective-permute-start.38) | collective-permute-done | bytes 1179680 | tf_op jit(solution)/shard_map/ppermute | solution.py:681
  452.6 2.5 collective-permute-start.39
  459.0 3.1 multiply_subtract_fusion
  462.1 2.0 copy.149
  467.4 2.0 copy.150
  469.4 2.0 copy.151
  474.1 16.8 %adam.4 = (f32[4,384,1536]{2,1,0:T(8,128)}, f32[4,384,1536]{2,1,0:T(8,128)}, f32[4,384,1536]{2,1,0:T(8,128)}, f32[4,1536,384]{2,1,0:T(8,128)}, f32[4,1536,384]{2,1,0:T(8,128)}, /*index=5*/f32[4,1536,384]{2,1,0:T(8,128)}) custom-call(s32[28]{0:T(128)} %stack.119.meta, bf16[1536,384]{1,0:T(8,128)(2,1)} %broadcast_select_fusion.ready.ready_two, ...), custom_call_target="tpu_custom_call" | custom-call | tf_op jit(solution)/shard_map/adam/pallas_call | solution.py:654
  490.9 17.0 %adam.5 = (f32[4,384,1536]{2,1,0:T(8,128)}, f32[4,384,1536]{2,1,0:T(8,128)}, f32[4,384,1536]{2,1,0:T(8,128)}, f32[4,1536,384]{2,1,0:T(8,128)}, f32[4,1536,384]{2,1,0:T(8,128)}, /*index=5*/f32[4,1536,384]{2,1,0:T(8,128)}) custom-call(s32[28]{0:T(128)} %stack.119.meta, ...), custom_call_target="tpu_custom_call", output_to_operand_aliasing={{0}: (11, {}), {1}: (12, {}), {2}: (13, {}), {3}: (14, {}),... | custom-call | tf_op jit(solution)/shard_map/adam/pallas_call | solution.py:654
  507.9 17.0 %adam.6 = (f32[4,384,1536]{2,1,0:T(8,128)}, f32[4,384,1536]{2,1,0:T(8,128)}, f32[4,384,1536]{2,1,0:T(8,128)}, f32[4,1536,384]{2,1,0:T(8,128)}, f32[4,1536,384]{2,1,0:T(8,128)}, /*index=5*/f32[4,1536,384]{2,1,0:T(8,128)}) custom-call(s32[28]{0:T(128)} %stack.119.meta, ...), custom_call_target="tpu_custom_call", output_to_operand_aliasing={{0}: (11, {}), {1}: (12, {}), {2}: (13, {}), {3}: (14, {}),... | custom-call | tf_op jit(solution)/shard_map/adam/pallas_call | solution.py:654
  524.9 17.0 %adam.7 = (f32[4,384,1536]{2,1,0:T(8,128)}, f32[4,384,1536]{2,1,0:T(8,128)}, f32[4,384,1536]{2,1,0:T(8,128)}, f32[4,1536,384]{2,1,0:T(8,128)}, f32[4,1536,384]{2,1,0:T(8,128)}, /*index=5*/f32[4,1536,384]{2,1,0:T(8,128)}) custom-call(s32[28]{0:T(128)} %stack.119.meta, ...), custom_call_target="tpu_custom_call", output_to_operand_aliasing={{0}: (11, {}), {1}: (12, {}), {2}: (13, {}), {3}: (14, {}),... | custom-call | tf_op jit(solution)/shard_map/adam/pallas_call | solution.py:654
  (224 shorter events, 72.8 us)
Async XLA Ops:
  0.7 26.6 %copy-start.47 = (s32[1,2048]{1,0:T(1,128)S(1)}, s32[1,2048]{1,0:T(1,128)}, u32[]{:S(2)}) copy-start(s32[1,2048]{1,0:T(1,128)} %param.25) | copy-start | bytes 24580
  4.3 38.1 %copy-start.19 = (bf16[48,1664]{1,0:T(8,128)(2,1)}, bf16[48,1664]{1,0:T(8,128)(2,1)S(1)}, u32[]{:S(2)}) copy-start(bf16[48,1664]{1,0:T(8,128)(2,1)S(1)} %concatenate.15.w0) | copy-start | bytes 479236
  4.3 13.2 %collective-permute-start.6 = (bf16[48,1664]{1,0:T(8,128)(2,1)S(1)}, bf16[48,1664]{1,0:T(8,128)(2,1)S(1)}, u32[]{:S(2)}, u32[]{:S(2)}) collective-permute-start(bf16[48,1664]{1,0:T(8,128)(2,1)S(1)} %concatenate.15.w0), channel_id=1, source_target_pairs={{0,4},{4,0},{8,12},{12,8},{16,20},{20,16},{24,28},{28,24},{1,5},{5... | collective-permute-start | bytes 479240 | tf_op jit(solution)/shard_map/ppermute | solution.py:677
  4.9 9.8 %collective-permute-start.5 = (bf16[48,1664]{1,0:T(8,128)(2,1)S(1)}, bf16[48,1664]{1,0:T(8,128)(2,1)S(1)}, u32[]{:S(2)}, u32[]{:S(2)}) collective-permute-start(bf16[48,1664]{1,0:T(8,128)(2,1)S(1)} %concatenate.15.w0), channel_id=1, source_target_pairs={{0,24},{4,28},{8,16},{12,20},{16,8},{20,12},{24,0},{28,4},{1,25},{... | collective-permute-start | bytes 479240 | tf_op jit(solution)/shard_map/ppermute | solution.py:673
  9.6 14.1 %collective-permute-start.4 = (bf16[48,1664]{1,0:T(8,128)(2,1)S(1)}, bf16[48,1664]{1,0:T(8,128)(2,1)S(1)}, u32[]{:S(2)}, u32[]{:S(2)}) collective-permute-start(bf16[48,1664]{1,0:T(8,128)(2,1)S(1)} %concatenate.15.w0), channel_id=1, source_target_pairs={{0,16},{4,20},{8,24},{12,28},{16,0},{20,4},{24,8},{28,12},{1,17},{... | collective-permute-start | bytes 479240 | tf_op jit(solution)/shard_map/ppermute | solution.py:673
  9.6 15.6 %collective-permute-start.3 = (bf16[48,1664]{1,0:T(8,128)(2,1)S(1)}, bf16[48,1664]{1,0:T(8,128)(2,1)S(1)}, u32[]{:S(2)}, u32[]{:S(2)}) collective-permute-start(bf16[48,1664]{1,0:T(8,128)(2,1)S(1)} %concatenate.15.w0), channel_id=1, source_target_pairs={{0,8},{4,12},{8,0},{12,4},{16,24},{20,28},{24,16},{28,20},{1,9},{5... | collective-permute-start | bytes 479240 | tf_op jit(solution)/shard_map/ppermute | solution.py:673
  14.7 12.1 %collective-permute-start.9 = (bf16[48,1664]{1,0:T(8,128)(2,1)S(1)}, bf16[48,1664]{1,0:T(8,128)(2,1)S(1)}, u32[]{:S(2)}, u32[]{:S(2)}) collective-permute-start(bf16[48,1664]{1,0:T(8,128)(2,1)S(1)} %collective-permute-done.5.w3), channel_id=1, source_target_pairs={{0,4},{4,0},{8,12},{12,8},{16,20},{20,16},{24,28},{28,24},{1,5},{5... | collective-permute-start | bytes 479240 | tf_op jit(solution)/shard_map/ppermute | solution.py:677
  14.8 27.7 %copy-start.3 = (bf16[528,384]{1,0:T(8,128)(2,1)}, bf16[528,384]{1,0:T(8,128)(2,1)S(1)}, u32[]{:S(2)}) copy-start(bf16[528,384]{1,0:T(8,128)(2,1)S(1)} %fusion.9.p0.i0.own) | copy-start | bytes 1216516
  14.8 26.1 %collective-permute-start.2 = (bf16[528,384]{1,0:T(8,128)(2,1)S(1)}, bf16[528,384]{1,0:T(8,128)(2,1)S(1)}, u32[]{:S(2)}, u32[]{:S(2)}) collective-permute-start(bf16[528,384]{1,0:T(8,128)(2,1)S(1)} %fusion.9.p0.i0.own), channel_id=1, source_target_pairs={{0,3},{1,2},{2,1},{3,0},{4,7},{5,6},{6,5},{7,4},{8,11},{9,10},{10,... | collective-permute-start | bytes 1216520 | tf_op jit(solution)/shard_map/ppermute | solution.py:669
  17.5 24.9 %collective-permute-start.1 = (bf16[528,384]{1,0:T(8,128)(2,1)S(1)}, bf16[528,384]{1,0:T(8,128)(2,1)S(1)}, u32[]{:S(2)}, u32[]{:S(2)}) collective-permute-start(bf16[528,384]{1,0:T(8,128)(2,1)S(1)} %fusion.9.p0.i0.own), channel_id=1, source_target_pairs={{0,2},{1,3},{2,0},{3,1},{4,6},{5,7},{6,4},{7,5},{8,10},{9,11},{10,... | collective-permute-start | bytes 1216520 | tf_op jit(solution)/shard_map/ppermute | solution.py:669
  23.7 18.8 %collective-permute-start = (bf16[528,384]{1,0:T(8,128)(2,1)S(1)}, bf16[528,384]{1,0:T(8,128)(2,1)S(1)}, u32[]{:S(2)}, u32[]{:S(2)}) collective-permute-start(bf16[528,384]{1,0:T(8,128)(2,1)S(1)} %fusion.9.p0.i0.own), channel_id=1, source_target_pairs={{0,1},{1,0},{2,3},{3,2},{4,5},{5,4},{6,7},{7,6},{8,9},{9,8},{10,11... | collective-permute-start | bytes 1216520 | tf_op jit(solution)/shard_map/ppermute | solution.py:669
  25.2 43.5 %collective-permute-start.15 = (bf16[512,384]{1,0:T(8,128)(2,1)S(1)}, bf16[512,384]{1,0:T(8,128)(2,1)S(1)}, u32[]{:S(2)}, u32[]{:S(2)}) collective-permute-start(bf16[512,384]{1,0:T(8,128)(2,1)S(1)} %bitcast.121), channel_id=1, source_target_pairs={{0,3},{1,2},{2,1},{3,0},{4,7},{5,6},{6,5},{7,4},{8,11},{9,10},{10,... | collective-permute-start | bytes 1179656 | tf_op jit(solution)/shard_map/ppermute | solution.py:669
  26.7 1.5 collective-permute-start.8
  28.3 12.0 %collective-permute-start.7 = (bf16[48,1664]{1,0:T(8,128)(2,1)S(1)}, bf16[48,1664]{1,0:T(8,128)(2,1)}, u32[]{:S(2)}, u32[]{:S(2)}) collective-permute-start(bf16[48,1664]{1,0:T(8,128)(2,1)S(1)} %collective-permute-done.3.w1), channel_id=1, source_target_pairs={{0,4},{4,0},{8,12},{12,8},{16,20},{20,16},{24,28},{28,24},{1,5},{5... | collective-permute-start | bytes 479240 | tf_op jit(solution)/shard_map/ppermute | solution.py:677
  40.3 32.7 %collective-permute-start.14 = (bf16[512,384]{1,0:T(8,128)(2,1)S(1)}, bf16[512,384]{1,0:T(8,128)(2,1)S(1)}, u32[]{:S(2)}, u32[]{:S(2)}) collective-permute-start(bf16[512,384]{1,0:T(8,128)(2,1)S(1)} %bitcast.122), channel_id=1, source_target_pairs={{0,2},{1,3},{2,0},{3,1},{4,6},{5,7},{6,4},{7,5},{8,10},{9,11},{10,... | collective-permute-start | bytes 1179656 | tf_op jit(solution)/shard_map/ppermute | solution.py:669
  40.9 32.2 %collective-permute-start.13 = (bf16[512,384]{1,0:T(8,128)(2,1)S(1)}, bf16[512,384]{1,0:T(8,128)(2,1)S(1)}, u32[]{:S(2)}, u32[]{:S(2)}) collective-permute-start(bf16[512,384]{1,0:T(8,128)(2,1)S(1)} %bitcast.123), channel_id=1, source_target_pairs={{0,1},{1,0},{2,3},{3,2},{4,5},{5,4},{6,7},{7,6},{8,9},{9,8},{10,11... | collective-permute-start | bytes 1179656 | tf_op jit(solution)/shard_map/ppermute | solution.py:669
  66.7 11.0 %collective-permute-start.12 = (bf16[512,384]{1,0:T(8,128)(2,1)}, bf16[512,384]{1,0:T(8,128)(2,1)S(1)}, u32[]{:S(2)}, u32[]{:S(2)}) collective-permute-start(bf16[512,384]{1,0:T(8,128)(2,1)} %get-tuple-element.68.m0), channel_id=1, source_target_pairs={{0,3},{1,2},{2,1},{3,0},{4,7},{5,6},{6,5},{7,4},{8,11},{9,10},{10,... | collective-permute-start | bytes 1179656 | tf_op jit(solution)/shard_map/ppermute | solution.py:669
  68.1 19.6 %collective-permute-start.11 = (bf16[512,384]{1,0:T(8,128)(2,1)}, bf16[512,384]{1,0:T(8,128)(2,1)S(1)}, u32[]{:S(2)}, u32[]{:S(2)}) collective-permute-start(bf16[512,384]{1,0:T(8,128)(2,1)} %get-tuple-element.68.m0), channel_id=1, source_target_pairs={{0,2},{1,3},{2,0},{3,1},{4,6},{5,7},{6,4},{7,5},{8,10},{9,11},{10,... | collective-permute-start | bytes 1179656 | tf_op jit(solution)/shard_map/ppermute | solution.py:669
  68.7 19.1 %collective-permute-start.10 = (bf16[512,384]{1,0:T(8,128)(2,1)}, bf16[512,384]{1,0:T(8,128)(2,1)S(1)}, u32[]{:S(2)}, u32[]{:S(2)}) collective-permute-start(bf16[512,384]{1,0:T(8,128)(2,1)} %get-tuple-element.68.m0), channel_id=1, source_target_pairs={{0,1},{1,0},{2,3},{3,2},{4,5},{5,4},{6,7},{7,6},{8,9},{9,8},{10,11... | collective-permute-start | bytes 1179656 | tf_op jit(solution)/shard_map/ppermute | solution.py:669
  145.8 2.9 collective-permute-start.50
  146.1 4.3 collective-permute-start.45
  146.4 5.7 %collective-permute-start.40 = (bf16[1536,384]{1,0:T(8,128)(2,1)S(1)}, bf16[1536,384]{1,0:T(8,128)(2,1)S(1)}, u32[]{:S(2)}, u32[]{:S(2)}) collective-permute-start(bf16[1536,384]{1,0:T(8,128)(2,1)S(1)} %get-tuple-element.230), channel_id=1, source_target_pairs={{0,4},{4,0},{8,12},{12,8},{16,20},{20,16},{24,28},{28,24},{1,5},{5... | collective-permute-start | bytes 3538952 | tf_op jit(solution)/shard_map/ppermute | solution.py:677
  146.6 7.2 %collective-permute-start.35 = (bf16[1536,384]{1,0:T(8,128)(2,1)S(1)}, bf16[1536,384]{1,0:T(8,128)(2,1)S(1)}, u32[]{:S(2)}, u32[]{:S(2)}) collective-permute-start(bf16[1536,384]{1,0:T(8,128)(2,1)S(1)} %get-tuple-element.231), channel_id=1, source_target_pairs={{0,4},{4,0},{8,12},{12,8},{16,20},{20,16},{24,28},{28,24},{1,5},{5... | collective-permute-start | bytes 3538952 | tf_op jit(solution)/shard_map/ppermute | solution.py:677
  155.7 90.0 %collective-permute-start.51 = (bf16[1536,384]{1,0:T(8,128)(2,1)}, bf16[1536,384]{1,0:T(8,128)(2,1)S(1)}, u32[]{:S(2)}, u32[]{:S(2)}) collective-permute-start(bf16[1536,384]{1,0:T(8,128)(2,1)} %get-tuple-element.224), channel_id=1, source_target_pairs={{0,8},{4,12},{24,16},{28,20},{1,9},{5,13},{25,17},{29,21},{2,10},{... | collective-permute-start | bytes 3538952 | tf_op jit(solution)/shard_map/ppermute | solution.py:681
  158.2 17.0 %collective-permute-start.21 = (bf16[512,384]{1,0:T(8,128)(2,1)S(1)}, bf16[512,384]{1,0:T(8,128)(2,1)S(1)}, u32[]{:S(2)}, u32[]{:S(2)}) collective-permute-start(bf16[512,384]{1,0:T(8,128)(2,1)S(1)} %get-tuple-element.235), channel_id=1, source_target_pairs={{0,3},{1,2},{2,1},{3,0},{4,7},{5,6},{6,5},{7,4},{8,11},{9,10},{10,... | collective-permute-start | bytes 1179656 | tf_op jit(solution)/shard_map/ppermute | solution.py:669
  165.2 17.6 %collective-permute-start.20 = (bf16[512,384]{1,0:T(8,128)(2,1)S(1)}, bf16[512,384]{1,0:T(8,128)(2,1)S(1)}, u32[]{:S(2)}, u32[]{:S(2)}) collective-permute-start(bf16[512,384]{1,0:T(8,128)(2,1)S(1)} %get-tuple-element.236), channel_id=1, source_target_pairs={{0,2},{1,3},{2,0},{3,1},{4,6},{5,7},{6,4},{7,5},{8,10},{9,11},{10,... | collective-permute-start | bytes 1179656 | tf_op jit(solution)/shard_map/ppermute | solution.py:669
  165.2 17.6 %collective-permute-start.19 = (bf16[512,384]{1,0:T(8,128)(2,1)S(1)}, bf16[512,384]{1,0:T(8,128)(2,1)S(1)}, u32[]{:S(2)}, u32[]{:S(2)}) collective-permute-start(bf16[512,384]{1,0:T(8,128)(2,1)S(1)} %get-tuple-element.237), channel_id=1, source_target_pairs={{0,1},{1,0},{2,3},{3,2},{4,5},{5,4},{6,7},{7,6},{8,9},{9,8},{10,11... | collective-permute-start | bytes 1179656 | tf_op jit(solution)/shard_map/ppermute | solution.py:669
  188.5 14.2 %collective-permute-start.24 = (bf16[576,384]{1,0:T(8,128)(2,1)}, bf16[576,384]{1,0:T(8,128)(2,1)S(1)}, u32[]{:S(2)}, u32[]{:S(2)}) collective-permute-start(bf16[576,384]{1,0:T(8,128)(2,1)} %get-tuple-element.77.s0), channel_id=1, source_target_pairs={{0,3},{1,2},{2,1},{3,0},{4,7},{5,6},{6,5},{7,4},{8,11},{9,10},{10,... | collective-permute-start | bytes 1327112 | tf_op jit(solution)/shard_map/ppermute | solution.py:669
  190.3 20.7 %collective-permute-start.23 = (bf16[576,384]{1,0:T(8,128)(2,1)}, bf16[576,384]{1,0:T(8,128)(2,1)S(1)}, u32[]{:S(2)}, u32[]{:S(2)}) collective-permute-start(bf16[576,384]{1,0:T(8,128)(2,1)} %get-tuple-element.77.s0), channel_id=1, source_target_pairs={{0,2},{1,3},{2,0},{3,1},{4,6},{5,7},{6,4},{7,5},{8,10},{9,11},{10,... | collective-permute-start | bytes 1327112 | tf_op jit(solution)/shard_map/ppermute | solution.py:669
  191.6 19.4 %collective-permute-start.22 = (bf16[576,384]{1,0:T(8,128)(2,1)}, bf16[576,384]{1,0:T(8,128)(2,1)S(1)}, u32[]{:S(2)}, u32[]{:S(2)}) collective-permute-start(bf16[576,384]{1,0:T(8,128)(2,1)} %get-tuple-element.77.s0), channel_id=1, source_target_pairs={{0,1},{1,0},{2,3},{3,2},{4,5},{5,4},{6,7},{7,6},{8,9},{9,8},{10,11... | collective-permute-start | bytes 1327112 | tf_op jit(solution)/shard_map/ppermute | solution.py:669
  192.0 81.0 %collective-permute-start.46 = (bf16[1536,384]{1,0:T(8,128)(2,1)}, bf16[1536,384]{1,0:T(8,128)(2,1)}, u32[]{:S(2)}, u32[]{:S(2)}) collective-permute-start(bf16[1536,384]{1,0:T(8,128)(2,1)} %get-tuple-element.225), channel_id=1, source_target_pairs={{0,8},{4,12},{24,16},{28,20},{1,9},{5,13},{25,17},{29,21},{2,10},{... | collective-permute-start | bytes 3538952 | tf_op jit(solution)/shard_map/ppermute | solution.py:681
  211.9 26.7 %copy-start.5 = (bf16[1536,384]{1,0:T(8,128)(2,1)S(1)}, bf16[1536,384]{1,0:T(8,128)(2,1)}, u32[]{:S(2)}) copy-start(bf16[1536,384]{1,0:T(8,128)(2,1)} %get-tuple-element.226) | copy-start | bytes 3538948
  238.6 41.2 %collective-permute-start.41 = (bf16[1536,384]{1,0:T(8,128)(2,1)S(1)}, bf16[1536,384]{1,0:T(8,128)(2,1)}, u32[]{:S(2)}, u32[]{:S(2)}) collective-permute-start(bf16[1536,384]{1,0:T(8,128)(2,1)S(1)} %copy-done.5), channel_id=1, source_target_pairs={{0,8},{4,12},{24,16},{28,20},{1,9},{5,13},{25,17},{29,21},{2,10},{... | collective-permute-start | bytes 3538952 | tf_op jit(solution)/shard_map/ppermute | solution.py:681
  243.7 8.1 %collective-permute-start.25 = (bf16[384,512]{1,0:T(8,128)(2,1)}, bf16[384,512]{1,0:T(8,128)(2,1)}, u32[]{:S(2)}, u32[]{:S(2)}) collective-permute-start(bf16[384,512]{1,0:T(8,128)(2,1)} %get-tuple-element.232), channel_id=1, source_target_pairs={{0,1},{1,0},{2,3},{3,2},{4,5},{5,4},{6,7},{7,6},{8,9},{9,8},{10,11... | collective-permute-start | bytes 1179656 | tf_op jit(solution)/shard_map/ppermute | solution.py:669
  244.3 13.9 %collective-permute-start.27 = (bf16[384,512]{1,0:T(8,128)(2,1)}, bf16[384,512]{1,0:T(8,128)(2,1)}, u32[]{:S(2)}, u32[]{:S(2)}) collective-permute-start(bf16[384,512]{1,0:T(8,128)(2,1)} %get-tuple-element.233), channel_id=1, source_target_pairs={{0,3},{1,2},{2,1},{3,0},{4,7},{5,6},{6,5},{7,4},{8,11},{9,10},{10,... | collective-permute-start | bytes 1179656 | tf_op jit(solution)/shard_map/ppermute | solution.py:669
  245.7 14.2 %collective-permute-start.26 = (bf16[384,512]{1,0:T(8,128)(2,1)}, bf16[384,512]{1,0:T(8,128)(2,1)}, u32[]{:S(2)}, u32[]{:S(2)}) collective-permute-start(bf16[384,512]{1,0:T(8,128)(2,1)} %get-tuple-element.234), channel_id=1, source_target_pairs={{0,2},{1,3},{2,0},{3,1},{4,6},{5,7},{6,4},{7,5},{8,10},{9,11},{10,... | collective-permute-start | bytes 1179656 | tf_op jit(solution)/shard_map/ppermute | solution.py:669
  251.7 89.1 %collective-permute-start.36 = (bf16[1536,384]{1,0:T(8,128)(2,1)S(1)}, bf16[1536,384]{1,0:T(8,128)(2,1)}, u32[]{:S(2)}, u32[]{:S(2)}) collective-permute-start(bf16[1536,384]{1,0:T(8,128)(2,1)S(1)} %get-tuple-element.227), channel_id=1, source_target_pairs={{0,8},{4,12},{24,16},{28,20},{1,9},{5,13},{25,17},{29,21},{2,10},{... | collective-permute-start | bytes 3538952 | tf_op jit(solution)/shard_map/ppermute | solution.py:681
  258.2 85.9 %collective-permute-start.52 = (bf16[1536,384]{1,0:T(8,128)(2,1)}, bf16[1536,384]{1,0:T(8,128)(2,1)}, u32[]{:S(2)}, u32[]{:S(2)}) collective-permute-start(bf16[1536,384]{1,0:T(8,128)(2,1)} %add.265), channel_id=1, source_target_pairs={{8,16},{12,20},{16,8},{20,12},{9,17},{13,21},{17,9},{21,13},{10,18... | collective-permute-start | bytes 3538952 | tf_op jit(solution)/shard_map/ppermute | solution.py:681
  261.5 17.2 %collective-permute-start.28 = (bf16[4,48,512]{2,1,0:T(8,128)(2,1)S(1)}, bf16[4,48,512]{2,1,0:T(8,128)(2,1)S(1)}, u32[]{:S(2)}, u32[]{:S(2)}) collective-permute-start(bf16[4,48,512]{2,1,0:T(8,128)(2,1)S(1)} %dynamic-slice_bitcast_fusion), channel_id=1, source_target_pairs={{0,4},{4,0},{8,12},{12,8},{16,20},{20,16},{24,28},{28,24},{1,5},{5... | collective-permute-start | bytes 589832 | tf_op jit(solution)/shard_map/ppermute | solution.py:677
  275.9 78.4 %collective-permute-start.47 = (bf16[1536,384]{1,0:T(8,128)(2,1)}, bf16[1536,384]{1,0:T(8,128)(2,1)}, u32[]{:S(2)}, u32[]{:S(2)}) collective-permute-start(bf16[1536,384]{1,0:T(8,128)(2,1)} %add.262), channel_id=1, source_target_pairs={{8,16},{12,20},{16,8},{20,12},{9,17},{13,21},{17,9},{21,13},{10,18... | collective-permute-start | bytes 3538952 | tf_op jit(solution)/shard_map/ppermute | solution.py:681
  278.6 12.3 %collective-permute-start.16 = (bf16[512,384]{1,0:T(8,128)(2,1)}, bf16[512,384]{1,0:T(8,128)(2,1)}, u32[]{:S(2)}, u32[]{:S(2)}) collective-permute-start(bf16[512,384]{1,0:T(8,128)(2,1)} %get-tuple-element.238), channel_id=1, source_target_pairs={{0,1},{1,0},{2,3},{3,2},{4,5},{5,4},{6,7},{7,6},{8,9},{9,8},{10,11... | collective-permute-start | bytes 1179656 | tf_op jit(solution)/shard_map/ppermute | solution.py:669
  279.8 19.9 %collective-permute-start.18 = (bf16[512,384]{1,0:T(8,128)(2,1)}, bf16[512,384]{1,0:T(8,128)(2,1)}, u32[]{:S(2)}, u32[]{:S(2)}) collective-permute-start(bf16[512,384]{1,0:T(8,128)(2,1)} %get-tuple-element.239), channel_id=1, source_target_pairs={{0,3},{1,2},{2,1},{3,0},{4,7},{5,6},{6,5},{7,4},{8,11},{9,10},{10,... | collective-permute-start | bytes 1179656 | tf_op jit(solution)/shard_map/ppermute | solution.py:669
  290.9 78.8 %collective-permute-start.42 = (bf16[1536,384]{1,0:T(8,128)(2,1)}, bf16[1536,384]{1,0:T(8,128)(2,1)}, u32[]{:S(2)}, u32[]{:S(2)}) collective-permute-start(bf16[1536,384]{1,0:T(8,128)(2,1)} %add.259), channel_id=1, source_target_pairs={{8,16},{12,20},{16,8},{20,12},{9,17},{13,21},{17,9},{21,13},{10,18... | collective-permute-start | bytes 3538952 | tf_op jit(solution)/shard_map/ppermute | solution.py:681
  299.7 4.1 collective-permute-start.29
  303.8 6.0 %collective-permute-start.31 = (bf16[48,512]{1,0:T(8,128)(2,1)S(1)}, bf16[48,512]{1,0:T(8,128)(2,1)S(1)}, u32[]{:S(2)}, u32[]{:S(2)}) collective-permute-start(bf16[48,512]{1,0:T(8,128)(2,1)S(1)} %get-tuple-element.246), channel_id=1, source_target_pairs={{0,24},{4,28},{8,16},{12,20},{16,8},{20,12},{24,0},{28,4},{1,25},{... | collective-permute-start | bytes 147464 | tf_op jit(solution)/shard_map/ppermute | solution.py:673
  309.8 34.3 %copy-start.44 = (bf16[48,512]{1,0:T(8,128)(2,1)}, bf16[48,512]{1,0:T(8,128)(2,1)S(1)}, u32[]{:S(2)}) copy-start(bf16[48,512]{1,0:T(8,128)(2,1)S(1)} %collective-permute-done.31) | copy-start | bytes 147460
  309.8 38.1 %collective-permute-start.30 = (bf16[48,512]{1,0:T(8,128)(2,1)S(1)}, bf16[48,512]{1,0:T(8,128)(2,1)S(1)}, u32[]{:S(2)}, u32[]{:S(2)}) collective-permute-start(bf16[48,512]{1,0:T(8,128)(2,1)S(1)} %get-tuple-element.247), channel_id=1, source_target_pairs={{0,16},{4,20},{8,24},{12,28},{16,0},{20,4},{24,8},{28,12},{1,17},{... | collective-permute-start | bytes 147464 | tf_op jit(solution)/shard_map/ppermute | solution.py:673
  340.8 10.8 %collective-permute-start.17 = (bf16[512,384]{1,0:T(8,128)(2,1)S(1)}, bf16[512,384]{1,0:T(8,128)(2,1)}, u32[]{:S(2)}, u32[]{:S(2)}) collective-permute-start(bf16[512,384]{1,0:T(8,128)(2,1)S(1)} %get-tuple-element.240), channel_id=1, source_target_pairs={{0,2},{1,3},{2,0},{3,1},{4,6},{5,7},{6,4},{7,5},{8,10},{9,11},{10,... | collective-permute-start | bytes 1179656 | tf_op jit(solution)/shard_map/ppermute | solution.py:669
  344.1 33.6 %collective-permute-start.37 = (bf16[1536,384]{1,0:T(8,128)(2,1)S(1)}, bf16[1536,384]{1,0:T(8,128)(2,1)}, u32[]{:S(2)}, u32[]{:S(2)}) collective-permute-start(bf16[1536,384]{1,0:T(8,128)(2,1)S(1)} %add.256), channel_id=1, source_target_pairs={{8,16},{12,20},{16,8},{20,12},{9,17},{13,21},{17,9},{21,13},{10,18... | collective-permute-start | bytes 3538952 | tf_op jit(solution)/shard_map/ppermute | solution.py:681
  348.5 32.6 %collective-permute-start.53 = (bf16[1536,384]{1,0:T(8,128)(2,1)S(1)}, bf16[1536,384]{1,0:T(8,128)(2,1)}, u32[]{:S(2)}, u32[]{:S(2)}) collective-permute-start(bf16[1536,384]{1,0:T(8,128)(2,1)S(1)} %add.266), channel_id=1, source_target_pairs={{8,0},{12,4},{16,24},{20,28},{9,1},{13,5},{17,25},{21,29},{10,2},{... | collective-permute-start | bytes 3538952 | tf_op jit(solution)/shard_map/ppermute | solution.py:681
  351.6 12.9 %collective-permute-start.34 = (bf16[48,512]{1,0:T(8,128)(2,1)}, bf16[48,512]{1,0:T(8,128)(2,1)}, u32[]{:S(2)}, u32[]{:S(2)}) collective-permute-start(bf16[48,512]{1,0:T(8,128)(2,1)} %fusion.14), channel_id=1, source_target_pairs={{0,3},{1,2},{2,1},{3,0},{4,7},{5,6},{6,5},{7,4},{8,11},{9,10},{10,... | collective-permute-start | bytes 147464 | tf_op jit(solution)/shard_map/ppermute | solution.py:669
  354.3 10.3 %collective-permute-start.33 = (bf16[48,512]{1,0:T(8,128)(2,1)}, bf16[48,512]{1,0:T(8,128)(2,1)}, u32[]{:S(2)}, u32[]{:S(2)}) collective-permute-start(bf16[48,512]{1,0:T(8,128)(2,1)} %fusion.14), channel_id=1, source_target_pairs={{0,2},{1,3},{2,0},{3,1},{4,6},{5,7},{6,4},{7,5},{8,10},{9,11},{10,... | collective-permute-start | bytes 147464 | tf_op jit(solution)/shard_map/ppermute | solution.py:669
  364.5 4.4 collective-permute-start.32
  364.6 37.4 %collective-permute-start.48 = (bf16[1536,384]{1,0:T(8,128)(2,1)S(1)}, bf16[1536,384]{1,0:T(8,128)(2,1)}, u32[]{:S(2)}, u32[]{:S(2)}) collective-permute-start(bf16[1536,384]{1,0:T(8,128)(2,1)S(1)} %add.263), channel_id=1, source_target_pairs={{8,0},{12,4},{16,24},{20,28},{9,1},{13,5},{17,25},{21,29},{10,2},{... | collective-permute-start | bytes 3538952 | tf_op jit(solution)/shard_map/ppermute | solution.py:681
  372.7 54.6 %collective-permute-start.43 = (bf16[1536,384]{1,0:T(8,128)(2,1)}, bf16[1536,384]{1,0:T(8,128)(2,1)}, u32[]{:S(2)}, u32[]{:S(2)}) collective-permute-start(bf16[1536,384]{1,0:T(8,128)(2,1)} %add.260), channel_id=1, source_target_pairs={{8,0},{12,4},{16,24},{20,28},{9,1},{13,5},{17,25},{21,29},{10,2},{... | collective-permute-start | bytes 3538952 | tf_op jit(solution)/shard_map/ppermute | solution.py:681
  377.8 77.4 %copy-start.8 = (f32[48,2048]{0,1:T(8,128)}, f32[48,2048]{0,1:T(8,128)S(1)}, u32[]{:S(2)}) copy-start(f32[48,2048]{0,1:T(8,128)S(1)} %convert_element_type.116) | copy-start | bytes 1179652
  379.7 72.7 %collective-permute-start.38 = (bf16[1536,384]{1,0:T(8,128)(2,1)S(1)}, bf16[1536,384]{1,0:T(8,128)(2,1)S(1)}, u32[]{:S(2)}, u32[]{:S(2)}) collective-permute-start(bf16[1536,384]{1,0:T(8,128)(2,1)S(1)} %add.257), channel_id=1, source_target_pairs={{8,0},{12,4},{16,24},{20,28},{9,1},{13,5},{17,25},{21,29},{10,2},{... | collective-permute-start | bytes 3538952 | tf_op jit(solution)/shard_map/ppermute | solution.py:681
  383.6 90.4 %collective-permute-start.54 = (bf16[1536,384]{1,0:T(8,128)(2,1)}, bf16[1536,384]{1,0:T(8,128)(2,1)}, u32[]{:S(2)}, u32[]{:S(2)}) collective-permute-start(bf16[1536,384]{1,0:T(8,128)(2,1)} %broadcast_select_fusion.ready.ready_two), channel_id=1, source_target_pairs={{0,4},{4,0},{8,12},{12,8},{16,20},{20,16},{24,28},{28,24},{1,5},{5... | collective-permute-start | bytes 3538952 | tf_op jit(solution)/shard_map/ppermute | solution.py:677
  403.5 87.5 %collective-permute-start.49 = (bf16[1536,384]{1,0:T(8,128)(2,1)S(1)}, bf16[1536,384]{1,0:T(8,128)(2,1)}, u32[]{:S(2)}, u32[]{:S(2)}) collective-permute-start(bf16[1536,384]{1,0:T(8,128)(2,1)S(1)} %broadcast_select_fusion.1.ready.ready_two), channel_id=1, source_target_pairs={{0,4},{4,0},{8,12},{12,8},{16,20},{20,16},{24,28},{28,24},{1,5},{5... | collective-permute-start | bytes 3538952 | tf_op jit(solution)/shard_map/ppermute | solution.py:677
  428.7 26.4 %copy-start.16 = (f32[48,384]{0,1:T(8,128)S(1)}, f32[48,384]{0,1:T(8,128)}, u32[]{:S(2)}) copy-start(f32[48,384]{0,1:T(8,128)} %copy.148) | copy-start | bytes 221188
  428.8 26.4 %copy-start.17 = (f32[48,384]{0,1:T(8,128)S(1)}, f32[48,384]{0,1:T(8,128)}, u32[]{:S(2)}) copy-start(f32[48,384]{0,1:T(8,128)} %copy.145) | copy-start | bytes 221188
  428.8 26.4 %copy-start.18 = (f32[48,384]{0,1:T(8,128)S(1)}, f32[48,384]{0,1:T(8,128)}, u32[]{:S(2)}) copy-start(f32[48,384]{0,1:T(8,128)} %copy.146) | copy-start | bytes 221188
  428.8 79.1 %collective-permute-start.44 = (bf16[1536,384]{1,0:T(8,128)(2,1)S(1)}, bf16[1536,384]{1,0:T(8,128)(2,1)}, u32[]{:S(2)}, u32[]{:S(2)}) collective-permute-start(bf16[1536,384]{1,0:T(8,128)(2,1)S(1)} %broadcast_select_fusion.2.ready.ready_two), channel_id=1, source_target_pairs={{0,4},{4,0},{8,12},{12,8},{16,20},{20,16},{24,28},{28,24},{1,5},{5... | collective-permute-start | bytes 3538952 | tf_op jit(solution)/shard_map/ppermute | solution.py:677
  452.6 72.2 %collective-permute-start.39 = (bf16[1536,384]{1,0:T(8,128)(2,1)S(1)}, bf16[1536,384]{1,0:T(8,128)(2,1)}, u32[]{:S(2)}, u32[]{:S(2)}) collective-permute-start(bf16[1536,384]{1,0:T(8,128)(2,1)S(1)} %broadcast_select_fusion.3.ready.ready_two), channel_id=1, source_target_pairs={{0,4},{4,0},{8,12},{12,8},{16,20},{20,16},{24,28},{28,24},{1,5},{5... | collective-permute-start | bytes 3538952 | tf_op jit(solution)/shard_map/ppermute | solution.py:677
  (41 other events, 428.6 us)
